TPU v7x, 512 devices: a whole 4x8x8 slice. The times are simulated.
512 devices in a mesh: gx: 64 (over z_lo, y, core), gy: 8 (over x, z_hi).
Axes of the slice: x: 4, y: 8, z: 8 (z_hi: 2, z_lo: 4; z = z_hi * 4 + z_lo), core: 2. Of those that a mesh axis runs over, the one named last changes fastest.
Arguments:
- velocity: float32 [3, 512, 256, 128], P(None, 'gx', 'gy'), may hold values from -6 to 6
- stress: float32 [6, 512, 256, 128], P(None, 'gx', 'gy'), may hold values from -6 to 6
- lame_lambda: bfloat16 [512, 256, 128], P('gx', 'gy'), may hold values from 0.5 to 1.5
- shear_modulus: bfloat16 [512, 256, 128], P('gx', 'gy'), may hold values from 0.29882812 to 1
- buoyancy: bfloat16 [512, 256, 128], P('gx', 'gy'), may hold values from 0.5 to 1.5
- source_p: bfloat16 [3, 512, 256, 128], P(None, 'gx', 'gy'), may hold values from -6 to 6
- source_s: bfloat16 [3, 512, 256, 128], P(None, 'gx', 'gy'), may hold values from -6 to 6
Outputs:
- image_p: float32 [512, 256, 128], P('gx', 'gy')
- image_s: float32 [512, 256, 128], P('gx', 'gy')
All inputs are finite; a program needn't handle non-finite values.
Results may differ from a plain program's by a relative error of at most 0.0003.
Values sent between devices are 32-bit elements; how exact they have to be, the bound alone decides.
A program may use at most 64 MiB of HBM per device.

v0:
```python
import math

import jax
import jax.numpy as jnp
from jax import lax
from jax.sharding import PartitionSpec as P

STEPS = 2


time_step = 0.2


def passed_along(block, axis, distance):
    devices = range(lax.axis_size(axis))
    route = [(i - distance, i) for i in devices if i - distance in devices]
    return lax.ppermute(block, axis, route)


def x_rims(planes, offset):
    return passed_along(planes, "gx", offset)


def y_rims(planes, offset):
    return passed_along(planes, "gy", offset)


def with_next(field, rim, which):
    length = field.shape[which]
    return jnp.concatenate([lax.slice_in_dim(field, 1, length, axis=which), rim], axis=which)


def with_prior(field, rim, which):
    length = field.shape[which]
    return jnp.concatenate([rim, lax.slice_in_dim(field, 0, length - 1, axis=which)], axis=which)


def zero_rim(field, which):
    return jnp.zeros_like(lax.slice_in_dim(field, 0, 1, axis=which))


def stress_step(velocity, stress, lame_value, shear_value):
    x_speed, y_speed, z_speed = (velocity[0], velocity[1], velocity[2])
    prior_x = x_rims(x_speed[None, -1:], 1)
    next_x = x_rims(jnp.stack([y_speed[:1], z_speed[:1]]), -1)
    prior_y = y_rims(y_speed[None, :, -1:], 1)
    next_y = y_rims(jnp.stack([x_speed[:, :1], z_speed[:, :1]]), -1)
    strain_x = x_speed - with_prior(x_speed, prior_x[0], 0)
    strain_y = y_speed - with_prior(y_speed, prior_y[0], 1)
    strain_z = z_speed - with_prior(z_speed, zero_rim(z_speed, 2), 2)
    volume = strain_x + strain_y + strain_z
    normal_x = stress[0] + time_step * (lame_value * volume + 2.0 * shear_value * strain_x)
    normal_y = stress[1] + time_step * (lame_value * volume + 2.0 * shear_value * strain_y)
    normal_z = stress[2] + time_step * (lame_value * volume + 2.0 * shear_value * strain_z)
    shear_xy = stress[3] + time_step * shear_value * (
        with_next(x_speed, next_y[0], 1) - x_speed + (with_next(y_speed, next_x[0], 0) - y_speed)
    )
    shear_xz = stress[4] + time_step * shear_value * (
        with_next(x_speed, zero_rim(x_speed, 2), 2)
        - x_speed
        + (with_next(z_speed, next_x[1], 0) - z_speed)
    )
    shear_yz = stress[5] + time_step * shear_value * (
        with_next(y_speed, zero_rim(y_speed, 2), 2)
        - y_speed
        + (with_next(z_speed, next_y[1], 1) - z_speed)
    )
    return jnp.stack([normal_x, normal_y, normal_z, shear_xy, shear_xz, shear_yz])


def velocity_step(velocity, stress, buoy_value):
    normal_x, normal_y, normal_z = (stress[0], stress[1], stress[2])
    shear_xy, shear_xz, shear_yz = (stress[3], stress[4], stress[5])
    next_x = x_rims(normal_x[None, :1], -1)
    prior_x = x_rims(jnp.stack([shear_xy[-1:], shear_xz[-1:]]), 1)
    next_y = y_rims(normal_y[None, :, :1], -1)
    prior_y = y_rims(jnp.stack([shear_xy[:, -1:], shear_yz[:, -1:]]), 1)
    x_speed = velocity[0] + time_step * buoy_value * (
        with_next(normal_x, next_x[0], 0)
        - normal_x
        + (shear_xy - with_prior(shear_xy, prior_y[0], 1))
        + (shear_xz - with_prior(shear_xz, zero_rim(shear_xz, 2), 2))
    )
    y_speed = velocity[1] + time_step * buoy_value * (
        shear_xy
        - with_prior(shear_xy, prior_x[0], 0)
        + (with_next(normal_y, next_y[0], 1) - normal_y)
        + (shear_yz - with_prior(shear_yz, zero_rim(shear_yz, 2), 2))
    )
    z_speed = velocity[2] + time_step * buoy_value * (
        shear_xz
        - with_prior(shear_xz, prior_x[1], 0)
        + (shear_yz - with_prior(shear_yz, prior_y[1], 1))
        + (with_next(normal_z, zero_rim(normal_z, 2), 2) - normal_z)
    )
    return jnp.stack([x_speed, y_speed, z_speed])


def phase_tables(length):
    positions = jnp.arange(length, dtype=jnp.int32)
    product = positions[:, None] * positions[None, :] % length
    phases = product.astype(jnp.float32) * (2.0 * math.pi / length)
    return (jnp.cos(phases), jnp.sin(phases))


def z_tables(z_cells, gy_count):
    quarter = z_cells // (2 * gy_count)
    width = gy_count * (quarter + 1)
    column = jnp.arange(width, dtype=jnp.int32)
    block = column // (quarter + 1)
    slot = column % (quarter + 1)
    waves = jnp.where(slot < quarter, block * quarter + slot, z_cells // 2)
    weight = jnp.where(
        slot < quarter, jnp.where(waves == 0, 1.0, 2.0), jnp.where(block == gy_count - 1, 1.0, 0.0)
    ).astype(jnp.float32)
    positions = jnp.arange(z_cells, dtype=jnp.int32)
    product = positions[:, None] * waves[None, :] % z_cells
    phases = product.astype(jnp.float32) * (2.0 * math.pi / z_cells)
    cos_fwd = jnp.cos(phases)
    sin_fwd = jnp.sin(phases)
    cos_back = jnp.transpose(cos_fwd) * weight[:, None]
    sin_back = jnp.transpose(sin_fwd) * weight[:, None]
    return (cos_fwd, sin_fwd, cos_back, sin_back, waves)


def contract(pattern, left, right):
    return jnp.einsum(pattern, left, right, precision=lax.Precision.HIGHEST)


def complex_sum(real_in, imag_in, cosine, sine, pattern, forward_sign):
    cos_real = contract(pattern, real_in, cosine)
    sin_imag = contract(pattern, imag_in, sine)
    cos_imag = contract(pattern, imag_in, cosine)
    sin_real = contract(pattern, real_in, sine)
    if forward_sign:
        return (cos_real + sin_imag, cos_imag - sin_real)
    return (cos_real - sin_imag, cos_imag + sin_real)


def signed_index(positions, length):
    half_length = length // 2
    signed = jnp.where(
        positions < half_length,
        positions,
        jnp.where(positions == half_length, 0, positions - length),
    )
    return signed.astype(jnp.float32)


def forward(velocity, cos_fwd, sin_fwd):
    x_cells, y_cells = (velocity.shape[1], velocity.shape[2])
    gx_count = lax.axis_size("gx")
    gy_count = lax.axis_size("gy")
    x_total = gx_count * x_cells
    y_total = gy_count * y_cells
    kept = cos_fwd.shape[1]
    z_part = kept // gy_count
    y_part = y_total // gx_count
    real_part = contract("cxyn,nk->ckxy", velocity, cos_fwd)
    imag_part = -contract("cxyn,nk->ckxy", velocity, sin_fwd)
    packed = jnp.stack([real_part, imag_part]).reshape(2, 3, 1, kept, x_cells * y_cells)
    arrived = lax.all_to_all(packed, "gy", split_axis=3, concat_axis=2, tiled=True)
    comp_count = arrived.shape[1]
    pieces = arrived.reshape(2, comp_count, gy_count, z_part, x_cells, y_cells)
    cos_y, sin_y = phase_tables(y_total)
    cos_y = cos_y.reshape(gy_count, y_cells, y_total)
    sin_y = sin_y.reshape(gy_count, y_cells, y_total)
    real_out, imag_out = complex_sum(pieces[0], pieces[1], cos_y, sin_y, "cgzxl,glk->ckzx", True)
    after_y = jnp.stack([real_out, imag_out]).reshape(2, comp_count, 1, y_total, z_part * x_cells)
    arrived = lax.all_to_all(after_y, "gx", split_axis=3, concat_axis=2, tiled=True)
    comp_count = arrived.shape[1]
    pieces = arrived.reshape(2, comp_count, gx_count, y_part, z_part, x_cells)
    cos_x, sin_x = phase_tables(x_total)
    cos_x = cos_x.reshape(gx_count, x_cells, x_total)
    sin_x = sin_x.reshape(gx_count, x_cells, x_total)
    real_out, imag_out = complex_sum(pieces[0], pieces[1], cos_x, sin_x, "cgazl,glk->cazk", True)
    return jnp.stack([real_out, imag_out])


def project(spectra, waves, z_total):
    y_part, z_part, x_total = (spectra.shape[2], spectra.shape[3], spectra.shape[4])
    gy_count = lax.axis_size("gy")
    y_total = y_part * lax.axis_size("gx")
    y_index = lax.axis_index("gx") * y_part + jnp.arange(y_part, dtype=jnp.int32)
    z_index = lax.dynamic_slice_in_dim(waves.reshape(gy_count, z_part), lax.axis_index("gy"), 1, 0)[
        0
    ]
    wave_x = signed_index(jnp.arange(x_total, dtype=jnp.int32), x_total)[None, None, :]
    wave_y = signed_index(y_index, y_total)[:, None, None]
    wave_z = signed_index(z_index, z_total)[None, :, None]
    inverse_norm = 1.0 / jnp.maximum(wave_x * wave_x + wave_y * wave_y + wave_z * wave_z, 1.0)
    radial = (
        wave_x * spectra[:, 0] + wave_y * spectra[:, 1] + wave_z * spectra[:, 2]
    ) * inverse_norm
    return jnp.stack([wave_x * radial, wave_y * radial, wave_z * radial], axis=1)


def inverse_fields(spectrum, x_cells, y_cells, z_cells, cos_back, sin_back):
    comp_count, y_part, z_part, x_total = (
        spectrum.shape[1],
        spectrum.shape[2],
        spectrum.shape[3],
        spectrum.shape[4],
    )
    gx_count = lax.axis_size("gx")
    gy_count = lax.axis_size("gy")
    y_total = y_part * gx_count
    norm_factor = 1.0 / (x_total * y_total * z_cells)
    cos_x, sin_x = phase_tables(x_total)
    real_part, imag_part = complex_sum(
        spectrum[0], spectrum[1], cos_x, sin_x, "cazk,kx->cxaz", False
    )
    packed = jnp.stack([real_part, imag_part]).reshape(2, comp_count, 1, x_total, y_part * z_part)
    arrived = lax.all_to_all(packed, "gx", split_axis=3, concat_axis=2, tiled=True)
    count_here = arrived.shape[1]
    pieces = arrived.reshape(2, count_here, gx_count, x_cells, y_part, z_part)
    cos_y, sin_y = phase_tables(y_total)
    cos_y = cos_y.reshape(gx_count, y_part, y_total)
    sin_y = sin_y.reshape(gx_count, y_part, y_total)
    real_out, imag_out = complex_sum(pieces[0], pieces[1], cos_y, sin_y, "cgxaz,gay->cyzx", False)
    middle = jnp.stack([real_out, imag_out]).reshape(2, count_here, 1, y_total, z_part * x_cells)
    arrived = lax.all_to_all(middle, "gy", split_axis=3, concat_axis=2, tiled=True)
    count_here = arrived.shape[1]
    pieces = arrived.reshape(2, count_here, gy_count, y_cells, z_part, x_cells)
    cos_z = cos_back.reshape(gy_count, z_part, z_cells)
    sin_z = sin_back.reshape(gy_count, z_part, z_cells)
    cos_real = contract("cgybx,gbn->cxyn", pieces[0], cos_z)
    sin_imag = contract("cgybx,gbn->cxyn", pieces[1], sin_z)
    return (cos_real - sin_imag) * norm_factor


def shards(velocity, stress, lame_lambda, shear_modulus, buoyancy, source_p, source_s):
    lame_value = lame_lambda.astype(jnp.float32)
    shear_value = shear_modulus.astype(jnp.float32)
    buoy_value = buoyancy.astype(jnp.float32)
    for step_index in range(STEPS):
        stress = stress_step(velocity, stress, lame_value, shear_value)
        velocity = velocity_step(velocity, stress, buoy_value)
    x_cells, y_cells, z_cells = (velocity.shape[1], velocity.shape[2], velocity.shape[3])
    gy_count = lax.axis_size("gy")
    cos_fwd, sin_fwd, cos_back, sin_back, waves = z_tables(z_cells, gy_count)
    spectra = forward(velocity, cos_fwd, sin_fwd)
    compression = project(spectra, waves, z_cells)
    p_field = inverse_fields(compression, x_cells, y_cells, z_cells, cos_back, sin_back)
    s_field = velocity - p_field
    image_p = jnp.sum(source_p.astype(jnp.float32) * p_field, axis=0)
    image_s = jnp.sum(source_s.astype(jnp.float32) * s_field, axis=0)
    return (image_p, image_s)


def solution(mesh):
    in_specs = (
        P(None, "gx", "gy", None),
        P(None, "gx", "gy", None),
        P("gx", "gy", None),
        P("gx", "gy", None),
        P("gx", "gy", None),
        P(None, "gx", "gy", None),
        P(None, "gx", "gy", None),
    )
    out_specs = (P("gx", "gy", None), P("gx", "gy", None))
    return jax.shard_map(shards, mesh=mesh, in_specs=in_specs, out_specs=out_specs, check_vma=False)
```

profile of v0, /device:TPU:64, one launch (start us, length us, event | category | flops | bytes accessed | tf_op | source)
XLA Modules:
  0.0 321.7 jit_solution(4998562081433264974)
XLA Ops:
  1.8 10.0 %collective-permute-start.1 = (f32[1,8,1,128]{3,1,2,0:T(8,128)S(1)}, f32[1,8,1,128]{3,1,2,0:T(8,128)S(1)}, u32[]{:S(2)}, u32[]{:S(2)}) collective-permute-start(f32[1,8,1,128]{3,1,2,0:T(8,128)S(1)} %bitcast.460), channel_id=1, source_target_pairs={{0,1},{1,2},{2,3},{3,4},{4,5},{5,6},{6,7},{8,9},{9,10},{10,11},{11... | collective-permute-start | bytes 12296 | tf_op jit(solution)/shard_map/ppermute | solution.py:17
  22.4 6.9 %collective-permute-done.3 = f32[2,8,1,128]{3,1,2,0:T(8,128)S(1)} collective-permute-done((f32[2,8,1,128]{3,1,2,0:T(8,128)S(1)}, f32[2,8,1,128]{3,1,2,0:T(8,128)S(1)}, u32[]{:S(2)}, u32[]{:S(2)}) %collective-permute-start.3) | collective-permute-done | bytes 8224 | tf_op jit(solution)/shard_map/ppermute | solution.py:17
  35.1 5.8 %collective-permute-start.2 = (f32[1,1,32,128]{3,2,1,0:T(8,128)S(1)}, f32[1,1,32,128]{3,2,1,0:T(8,128)S(1)}, u32[]{:S(2)}, u32[]{:S(2)}) collective-permute-start(f32[1,1,32,128]{3,2,1,0:T(8,128)S(1)} %slice_bitcast_fusion.28), channel_id=1, source_target_pairs={{8,0},{16,8},{24,16},{32,24},{40,32},{48,40},{56,48},{64,56},{72,6... | collective-permute-start | bytes 49160 | tf_op jit(solution)/shard_map/ppermute | solution.py:17
  43.8 6.4 %collective-permute-done.8 = f32[1,8,1,128]{3,1,2,0:T(8,128)S(1)} collective-permute-done((f32[1,8,1,128]{3,1,2,0:T(8,128)S(1)}, f32[1,8,1,128]{3,1,2,0:T(8,128)S(1)}, u32[]{:S(2)}, u32[]{:S(2)}) %collective-permute-start.8) | collective-permute-done | bytes 4128 | tf_op jit(solution)/shard_map/ppermute | solution.py:17
  52.6 8.5 %collective-permute-start.9 = (f32[1,8,1,128]{3,1,2,0:T(8,128)S(1)}, f32[1,8,1,128]{3,1,2,0:T(8,128)S(1)}, u32[]{:S(2)}, u32[]{:S(2)}) collective-permute-start(f32[1,8,1,128]{3,1,2,0:T(8,128)S(1)} %bitcast.461), channel_id=1, source_target_pairs={{0,1},{1,2},{2,3},{3,4},{4,5},{5,6},{6,7},{8,9},{9,10},{10,11},{11... | collective-permute-start | bytes 12296 | tf_op jit(solution)/shard_map/ppermute | solution.py:17
  63.3 5.0 %collective-permute-done.6 = f32[1,1,32,128]{3,2,1,0:T(8,128)S(1)} collective-permute-done((f32[1,1,32,128]{3,2,1,0:T(8,128)S(1)}, f32[1,1,32,128]{3,2,1,0:T(8,128)S(1)}, u32[]{:S(2)}, u32[]{:S(2)}) %collective-permute-start.6) | collective-permute-done | bytes 16416 | tf_op jit(solution)/shard_map/ppermute | solution.py:17
  68.7 5.6 %collective-permute-start.13 = (f32[2,8,1,128]{3,1,2,0:T(8,128)S(1)}, f32[2,8,1,128]{3,1,2,0:T(8,128)S(1)}, u32[]{:S(2)}, u32[]{:S(2)}) collective-permute-start(f32[2,8,1,128]{3,1,2,0:T(8,128)S(1)} %pad_maximum_fusion.15), channel_id=1, source_target_pairs={{0,1},{1,2},{2,3},{3,4},{4,5},{5,6},{6,7},{8,9},{9,10},{10,11},{11... | collective-permute-start | bytes 24584 | tf_op jit(solution)/shard_map/ppermute | solution.py:17
  77.8 5.8 %collective-permute-start.10 = (f32[1,1,32,128]{3,2,1,0:T(8,128)S(1)}, f32[1,1,32,128]{3,2,1,0:T(8,128)S(1)}, u32[]{:S(2)}, u32[]{:S(2)}) collective-permute-start(f32[1,1,32,128]{3,2,1,0:T(8,128)S(1)} %slice_bitcast_fusion.20), channel_id=1, source_target_pairs={{8,0},{16,8},{24,16},{32,24},{40,32},{48,40},{56,48},{64,56},{72,6... | collective-permute-start | bytes 49160 | tf_op jit(solution)/shard_map/ppermute | solution.py:17
  89.0 9.3 %all-to-all-start = ((f32[2,3,1,72,256]{4,0,2,1,3:T(2,128)}), f32[2,3,1,72,256]{4,0,2,1,3:T(2,128)S(1)}, u32[]{:S(2)}, u32[]{:S(2)}) async-start(f32[2,3,1,72,256]{4,0,2,1,3:T(2,128)} %pad_maximum_fusion.2), calls=%async_computation | async-start | bytes 884736 | tf_op jit(solution)/shard_map/all_to_all | solution.py:162
  98.4 13.9 %all-to-all-done = f32[2,3,1,72,256]{4,0,2,1,3:T(2,128)S(1)} async-done(((f32[2,3,1,72,256]{4,0,2,1,3:T(2,128)}), f32[2,3,1,72,256]{4,0,2,1,3:T(2,128)S(1)}, u32[]{:S(2)}, u32[]{:S(2)}) %all-to-all-start) | async-done | bytes 442400 | tf_op jit(solution)/shard_map/all_to_all | solution.py:162
  128.1 8.0 %all-to-all-start.1 = ((f32[2,3,1,256,72]{4,2,1,0,3:T(1,128)}), f32[2,3,1,256,72]{4,2,1,0,3:T(1,128)S(1)}, u32[]{:S(2)}, u32[]{:S(2)}) async-start(f32[2,3,1,256,72]{4,2,1,0,3:T(1,128)} %copy.142), calls=%async_computation.1 | async-start | bytes 1572864 | tf_op jit(solution)/shard_map/all_to_all | solution.py:170
  136.3 21.7 %all-to-all-done.1 = f32[2,3,1,256,72]{4,2,1,0,3:T(1,128)S(1)} async-done(((f32[2,3,1,256,72]{4,2,1,0,3:T(1,128)}), f32[2,3,1,256,72]{4,2,1,0,3:T(1,128)S(1)}, u32[]{:S(2)}, u32[]{:S(2)}) %all-to-all-start.1) | async-done | bytes 442400 | tf_op jit(solution)/shard_map/all_to_all | solution.py:170
  164.1 5.4 %copy.146 = f32[3,64,4,9,8]{1,3,4,2,0:T(8,128)S(1)} copy(f32[3,64,4,9,8]{4,3,0,2,1:T(8,128)} %reshape.522) | data formatting | bytes 442368 | tf_op jit(solution)/shard_map/squeeze | solution.py:176
  173.2 5.6 %copy.144 = f32[3,64,4,9,8]{1,3,4,2,0:T(8,128)S(1)} copy(f32[3,64,4,9,8]{4,3,0,2,1:T(8,128)} %reshape.521) | data formatting | bytes 442368 | tf_op jit(solution)/shard_map/squeeze | solution.py:176
  178.9 4.9 %convolution_bitcast_fusion.2 = f32[3,4,9,512]{3,2,1,0:T(8,128)S(1)} fusion(f32[3,64,4,9,8]{1,3,4,2,0:T(8,128)S(1)} %copy.146, s32[64,8]{0,1:T(8,128)S(1)} %multiply_add_fusion), kind=kOutput, calls=%fused_computation.20 | convolution fusion | flops 343408640 | bytes 444416 | tf_op jit(solution)/shard_map/cgazl,glk->cazk/dot_general | solution.py:127
  188.7 5.3 %fusion.49 = f32[1,3,4,9,512]{4,3,2,1,0:T(8,128)S(1)} fusion(f32[3,4,9,512]{3,2,1,0:T(8,128)S(1)} %convolution_bitcast_fusion.2, f32[3,64,4,9,8]{1,3,4,2,0:T(8,128)S(1)} %copy.144, s32[64,8]{0,1:T(8,128)S(1)} %multiply_add_fusion), kind=kOutput, calls=%fused_computation.46 | convolution fusion | flops 343463936 | bytes 665600 | tf_op jit(solution)/shard_map/cgazl,glk->cazk/dot_general | solution.py:127
  199.2 5.1 %fusion.71 = f32[512,3,4,9]{0,3,2,1:T(8,128)S(1)} fusion(f32[2,3,4,9,512]{4,3,2,1,0:T(8,128)S(1)} %pad_maximum_fusion), kind=kOutput, calls=%fused_computation.62 | convolution fusion | flops 343408640 | bytes 614400 | tf_op jit(solution)/shard_map/cazk,kx->cxaz/dot_general | solution.py:127
  204.3 5.3 %fusion.69 = f32[512,3,4,9]{0,3,2,1:T(8,128)S(1)} fusion(f32[2,3,4,9,512]{4,3,2,1,0:T(8,128)S(1)} %pad_maximum_fusion), kind=kOutput, calls=%fused_computation.60 | convolution fusion | flops 343408640 | bytes 614400 | tf_op jit(solution)/shard_map/cazk,kx->cxaz/dot_general | solution.py:127
  209.6 5.2 %fusion.43 = f32[3,512,4,9]{1,3,2,0:T(8,128)S(1)} fusion(f32[512,3,4,9]{0,3,2,1:T(8,128)S(1)} %fusion.71, f32[2,3,4,9,512]{4,3,2,1,0:T(8,128)S(1)} %pad_maximum_fusion), kind=kOutput, calls=%fused_computation.35 | convolution fusion | flops 343463936 | bytes 1007616 | tf_op jit(solution)/shard_map/cazk,kx->cxaz/dot_general | solution.py:127
  215.0 5.2 %fusion.42 = f32[3,512,4,9]{1,3,2,0:T(8,128)S(1)} fusion(f32[512,3,4,9]{0,3,2,1:T(8,128)S(1)} %fusion.69, f32[2,3,4,9,512]{4,3,2,1,0:T(8,128)S(1)} %pad_maximum_fusion), kind=kOutput, calls=%fused_computation.33 | convolution fusion | flops 343463936 | bytes 1007616 | tf_op jit(solution)/shard_map/cazk,kx->cxaz/dot_general | solution.py:127
  225.6 7.4 %all-to-all-start.2 = ((f32[64,1,1728]{2,1,0:T(1,128)}), f32[64,1,1728]{2,1,0:T(1,128)S(1)}, u32[]{:S(2)}, u32[]{:S(2)}) async-start(f32[64,1,1728]{2,1,0:T(1,128)} %reshape.531), calls=%async_computation.2 | async-start | bytes 917504 | tf_op jit(solution)/shard_map/all_to_all | solution.py:214
  233.0 15.2 %all-to-all-done.2 = f32[64,1,1728]{2,1,0:T(1,128)S(1)} async-done(((f32[64,1,1728]{2,1,0:T(1,128)}), f32[64,1,1728]{2,1,0:T(1,128)S(1)}, u32[]{:S(2)}, u32[]{:S(2)}) %all-to-all-start.2) | async-done | bytes 442400 | tf_op jit(solution)/shard_map/all_to_all | solution.py:214
  253.2 6.2 %slice_reduce_fusion.1 = (f32[3,512,36]{2,0,1:T(4,128)}, f32[3,512,36]{2,0,1:T(4,128)}) fusion(f32[2,3,1,512,36]{4,0,2,1,3:T(2,128)S(1)} %bitcast.413), kind=kLoop, calls=%fused_computation.79 | loop fusion | bytes 884736 | tf_op jit(solution)/shard_map/slice | solution.py:220
  287.0 26.1 %all-to-all-done.3 = f32[2,3,1,256,72]{4,2,1,0,3:T(1,128)S(1)} async-done(((f32[2,3,1,256,72]{4,2,1,0,3:T(1,128)}), f32[2,3,1,256,72]{4,2,1,0,3:T(1,128)S(1)}, u32[]{:S(2)}, u32[]{:S(2)}) %all-to-all-start.3) | async-done | bytes 442400 | tf_op jit(solution)/shard_map/all_to_all | solution.py:222
  (176 shorter events, 116.1 us)
Async XLA Ops:
  0.6 28.7 %copy-start = (f32[3,8,32,128]{3,2,1,0:T(8,128)S(1)}, f32[3,8,32,128]{3,2,1,0:T(8,128)}, u32[]{:S(2)}) copy-start(f32[3,8,32,128]{3,2,1,0:T(8,128)} %param.7) | copy-start | bytes 1179652
  0.6 28.7 %copy-start.3 = (bf16[8,32,128]{2,1,0:T(8,128)(2,1)S(1)}, bf16[8,32,128]{2,1,0:T(8,128)(2,1)}, u32[]{:S(2)}) copy-start(bf16[8,32,128]{2,1,0:T(8,128)(2,1)} %param.10) | copy-start | bytes 196612
  0.7 28.7 %copy-start.5 = (f32[6,8,32,128]{3,2,1,0:T(8,128)S(1)}, f32[6,8,32,128]{3,2,1,0:T(8,128)}, u32[]{:S(2)}) copy-start(f32[6,8,32,128]{3,2,1,0:T(8,128)} %param.8) | copy-start | bytes 2359300
  1.8 27.6 %copy-start.6 = (bf16[8,32,128]{2,1,0:T(8,128)(2,1)S(1)}, bf16[8,32,128]{2,1,0:T(8,128)(2,1)}, u32[]{:S(2)}) copy-start(bf16[8,32,128]{2,1,0:T(8,128)(2,1)} %param.9) | copy-start | bytes 196612
  1.8 27.6 %collective-permute-start.1 = (f32[1,8,1,128]{3,1,2,0:T(8,128)S(1)}, f32[1,8,1,128]{3,1,2,0:T(8,128)S(1)}, u32[]{:S(2)}, u32[]{:S(2)}) collective-permute-start(f32[1,8,1,128]{3,1,2,0:T(8,128)S(1)} %bitcast.460), channel_id=1, source_target_pairs={{0,1},{1,2},{2,3},{3,4},{4,5},{5,6},{6,7},{8,9},{9,10},{10,11},{11... | collective-permute-start | bytes 12296 | tf_op jit(solution)/shard_map/ppermute | solution.py:17
  12.6 16.7 %collective-permute-start.4 = (f32[2,1,32,128]{3,2,1,0:T(8,128)S(1)}, f32[2,1,32,128]{3,2,1,0:T(8,128)S(1)}, u32[]{:S(2)}, u32[]{:S(2)}) collective-permute-start(f32[2,1,32,128]{3,2,1,0:T(8,128)S(1)} %stack.134), channel_id=1, source_target_pairs={{8,0},{16,8},{24,16},{32,24},{40,32},{48,40},{56,48},{64,56},{72,6... | collective-permute-start | bytes 98312 | tf_op jit(solution)/shard_map/ppermute | solution.py:17
  17.9 11.6 %collective-permute-start = (f32[1,1,32,128]{3,2,1,0:T(8,128)S(1)}, f32[1,1,32,128]{3,2,1,0:T(8,128)S(1)}, u32[]{:S(2)}, u32[]{:S(2)}) collective-permute-start(f32[1,1,32,128]{3,2,1,0:T(8,128)S(1)} %slice.326), channel_id=1, source_target_pairs={{0,8},{8,16},{16,24},{24,32},{32,40},{40,48},{48,56},{56,64},{64,7... | collective-permute-start | bytes 49160 | tf_op jit(solution)/shard_map/ppermute | solution.py:17
  19.8 9.5 %collective-permute-start.3 = (f32[2,8,1,128]{3,1,2,0:T(8,128)S(1)}, f32[2,8,1,128]{3,1,2,0:T(8,128)S(1)}, u32[]{:S(2)}, u32[]{:S(2)}) collective-permute-start(f32[2,8,1,128]{3,1,2,0:T(8,128)S(1)} %pad_maximum_fusion.12), channel_id=1, source_target_pairs={{1,0},{2,1},{3,2},{4,3},{5,4},{6,5},{7,6},{9,8},{10,9},{11,10},{12... | collective-permute-start | bytes 24584 | tf_op jit(solution)/shard_map/ppermute | solution.py:17
  29.8 12.3 %collective-permute-start.5 = (f32[2,8,1,128]{3,1,2,0:T(8,128)S(1)}, f32[2,8,1,128]{3,1,2,0:T(8,128)S(1)}, u32[]{:S(2)}, u32[]{:S(2)}) collective-permute-start(f32[2,8,1,128]{3,1,2,0:T(8,128)S(1)} %pad_maximum_fusion.13), channel_id=1, source_target_pairs={{0,1},{1,2},{2,3},{3,4},{4,5},{5,6},{6,7},{8,9},{9,10},{10,11},{11... | collective-permute-start | bytes 24584 | tf_op jit(solution)/shard_map/ppermute | solution.py:17
  33.2 9.0 %collective-permute-start.7 = (f32[2,1,32,128]{3,2,1,0:T(8,128)S(1)}, f32[2,1,32,128]{3,2,1,0:T(8,128)S(1)}, u32[]{:S(2)}, u32[]{:S(2)}) collective-permute-start(f32[2,1,32,128]{3,2,1,0:T(8,128)S(1)} %pad_maximum_fusion.9), channel_id=1, source_target_pairs={{0,8},{8,16},{16,24},{24,32},{32,40},{40,48},{48,56},{56,64},{64,7... | collective-permute-start | bytes 98312 | tf_op jit(solution)/shard_map/ppermute | solution.py:17
  35.1 7.2 %collective-permute-start.2 = (f32[1,1,32,128]{3,2,1,0:T(8,128)S(1)}, f32[1,1,32,128]{3,2,1,0:T(8,128)S(1)}, u32[]{:S(2)}, u32[]{:S(2)}) collective-permute-start(f32[1,1,32,128]{3,2,1,0:T(8,128)S(1)} %slice_bitcast_fusion.28), channel_id=1, source_target_pairs={{8,0},{16,8},{24,16},{32,24},{40,32},{48,40},{56,48},{64,56},{72,6... | collective-permute-start | bytes 49160 | tf_op jit(solution)/shard_map/ppermute | solution.py:17
  40.8 9.4 %collective-permute-start.8 = (f32[1,8,1,128]{3,1,2,0:T(8,128)S(1)}, f32[1,8,1,128]{3,1,2,0:T(8,128)S(1)}, u32[]{:S(2)}, u32[]{:S(2)}) collective-permute-start(f32[1,8,1,128]{3,1,2,0:T(8,128)S(1)} %bitcast.459), channel_id=1, source_target_pairs={{1,0},{2,1},{3,2},{4,3},{5,4},{6,5},{7,6},{9,8},{10,9},{11,10},{12... | collective-permute-start | bytes 12296 | tf_op jit(solution)/shard_map/ppermute | solution.py:17
  42.5 20.7 %collective-permute-start.11 = (f32[2,8,1,128]{3,1,2,0:T(8,128)S(1)}, f32[2,8,1,128]{3,1,2,0:T(8,128)S(1)}, u32[]{:S(2)}, u32[]{:S(2)}) collective-permute-start(f32[2,8,1,128]{3,1,2,0:T(8,128)S(1)} %pad_maximum_fusion.14), channel_id=1, source_target_pairs={{1,0},{2,1},{3,2},{4,3},{5,4},{6,5},{7,6},{9,8},{10,9},{11,10},{12... | collective-permute-start | bytes 24584 | tf_op jit(solution)/shard_map/ppermute | solution.py:17
  50.7 12.6 %collective-permute-start.12 = (f32[2,1,32,128]{3,2,1,0:T(8,128)S(1)}, f32[2,1,32,128]{3,2,1,0:T(8,128)S(1)}, u32[]{:S(2)}, u32[]{:S(2)}) collective-permute-start(f32[2,1,32,128]{3,2,1,0:T(8,128)S(1)} %pad_maximum_fusion.10), channel_id=1, source_target_pairs={{8,0},{16,8},{24,16},{32,24},{40,32},{48,40},{56,48},{64,56},{72,6... | collective-permute-start | bytes 98312 | tf_op jit(solution)/shard_map/ppermute | solution.py:17
  52.6 10.7 %collective-permute-start.9 = (f32[1,8,1,128]{3,1,2,0:T(8,128)S(1)}, f32[1,8,1,128]{3,1,2,0:T(8,128)S(1)}, u32[]{:S(2)}, u32[]{:S(2)}) collective-permute-start(f32[1,8,1,128]{3,1,2,0:T(8,128)S(1)} %bitcast.461), channel_id=1, source_target_pairs={{0,1},{1,2},{2,3},{3,4},{4,5},{5,6},{6,7},{8,9},{9,10},{10,11},{11... | collective-permute-start | bytes 12296 | tf_op jit(solution)/shard_map/ppermute | solution.py:17
  61.1 7.2 %collective-permute-start.6 = (f32[1,1,32,128]{3,2,1,0:T(8,128)S(1)}, f32[1,1,32,128]{3,2,1,0:T(8,128)S(1)}, u32[]{:S(2)}, u32[]{:S(2)}) collective-permute-start(f32[1,1,32,128]{3,2,1,0:T(8,128)S(1)} %slice_bitcast_fusion.25), channel_id=1, source_target_pairs={{0,8},{8,16},{16,24},{24,32},{32,40},{40,48},{48,56},{56,64},{64,7... | collective-permute-start | bytes 49160 | tf_op jit(solution)/shard_map/ppermute | solution.py:17
  68.7 14.8 %collective-permute-start.13 = (f32[2,8,1,128]{3,1,2,0:T(8,128)S(1)}, f32[2,8,1,128]{3,1,2,0:T(8,128)S(1)}, u32[]{:S(2)}, u32[]{:S(2)}) collective-permute-start(f32[2,8,1,128]{3,1,2,0:T(8,128)S(1)} %pad_maximum_fusion.15), channel_id=1, source_target_pairs={{0,1},{1,2},{2,3},{3,4},{4,5},{5,6},{6,7},{8,9},{9,10},{10,11},{11... | collective-permute-start | bytes 24584 | tf_op jit(solution)/shard_map/ppermute | solution.py:17
  74.4 9.1 %collective-permute-start.14 = (f32[2,1,32,128]{3,2,1,0:T(8,128)S(1)}, f32[2,1,32,128]{3,2,1,0:T(8,128)S(1)}, u32[]{:S(2)}, u32[]{:S(2)}) collective-permute-start(f32[2,1,32,128]{3,2,1,0:T(8,128)S(1)} %pad_maximum_fusion.11), channel_id=1, source_target_pairs={{0,8},{8,16},{16,24},{24,32},{32,40},{40,48},{48,56},{56,64},{64,7... | collective-permute-start | bytes 98312 | tf_op jit(solution)/shard_map/ppermute | solution.py:17
  76.4 9.4 %collective-permute-start.15 = (f32[1,8,1,128]{3,1,2,0:T(8,128)S(1)}, f32[1,8,1,128]{3,1,2,0:T(8,128)S(1)}, u32[]{:S(2)}, u32[]{:S(2)}) collective-permute-start(f32[1,8,1,128]{3,1,2,0:T(8,128)S(1)} %bitcast.462), channel_id=1, source_target_pairs={{1,0},{2,1},{3,2},{4,3},{5,4},{6,5},{7,6},{9,8},{10,9},{11,10},{12... | collective-permute-start | bytes 12296 | tf_op jit(solution)/shard_map/ppermute | solution.py:17
  77.8 8.1 %collective-permute-start.10 = (f32[1,1,32,128]{3,2,1,0:T(8,128)S(1)}, f32[1,1,32,128]{3,2,1,0:T(8,128)S(1)}, u32[]{:S(2)}, u32[]{:S(2)}) collective-permute-start(f32[1,1,32,128]{3,2,1,0:T(8,128)S(1)} %slice_bitcast_fusion.20), channel_id=1, source_target_pairs={{8,0},{16,8},{24,16},{32,24},{40,32},{48,40},{56,48},{64,56},{72,6... | collective-permute-start | bytes 49160 | tf_op jit(solution)/shard_map/ppermute | solution.py:17
  89.0 23.3 %all-to-all-start = ((f32[2,3,1,72,256]{4,0,2,1,3:T(2,128)}), f32[2,3,1,72,256]{4,0,2,1,3:T(2,128)S(1)}, u32[]{:S(2)}, u32[]{:S(2)}) async-start(f32[2,3,1,72,256]{4,0,2,1,3:T(2,128)} %pad_maximum_fusion.2), calls=%async_computation | async-start | bytes 884736 | tf_op jit(solution)/shard_map/all_to_all | solution.py:162
  128.1 29.9 %all-to-all-start.1 = ((f32[2,3,1,256,72]{4,2,1,0,3:T(1,128)}), f32[2,3,1,256,72]{4,2,1,0,3:T(1,128)S(1)}, u32[]{:S(2)}, u32[]{:S(2)}) async-start(f32[2,3,1,256,72]{4,2,1,0,3:T(1,128)} %copy.142), calls=%async_computation.1 | async-start | bytes 1572864 | tf_op jit(solution)/shard_map/all_to_all | solution.py:170
  225.6 22.6 %all-to-all-start.2 = ((f32[64,1,1728]{2,1,0:T(1,128)}), f32[64,1,1728]{2,1,0:T(1,128)S(1)}, u32[]{:S(2)}, u32[]{:S(2)}) async-start(f32[64,1,1728]{2,1,0:T(1,128)} %reshape.531), calls=%async_computation.2 | async-start | bytes 917504 | tf_op jit(solution)/shard_map/all_to_all | solution.py:214
  283.3 29.8 %all-to-all-start.3 = ((f32[2,3,1,256,72]{4,2,1,0,3:T(1,128)}), f32[2,3,1,256,72]{4,2,1,0,3:T(1,128)S(1)}, u32[]{:S(2)}, u32[]{:S(2)}) async-start(f32[2,3,1,256,72]{4,2,1,0,3:T(1,128)} %copy.160), calls=%async_computation.3 | async-start | bytes 1572864 | tf_op jit(solution)/shard_map/all_to_all | solution.py:222
  (5 other events, 29.9 us)
where the time goes:
time: 327 us; the launch traced here: 322 us
  waiting for transfers between devices  97.5 us (30%)
  starting transfers between devices  86.5 us (26%)
  matrix products  70 us (21%)
  local copies, waits for them, and re-layouts  60.5 us (19%)
  other arithmetic  5.12 us (2%)
    dot_general x20, matrix products, contract(): return jnp.einsum(pattern, left, right, precision=lax.Precision.HIGHEST)  70 us
    ppermute x16, starting transfers between devices, passed_along(): return lax.ppermute(block, axis, route)  58.2 us
    all_to_all x1, waiting for transfers between devices, inverse_fields(): lax.all_to_all(middle, 'gy', split_axis=3, concat_axis=2, tiled=True)  26.1 us
    all_to_all x1, waiting for transfers between devices, forward(): lax.all_to_all(after_y, 'gx', split_axis=3, concat_axis=2, tiled=True)  21.7 us
    ppermute x16, waiting for transfers between devices, passed_along(): return lax.ppermute(block, axis, route)  20.6 us
    all_to_all x1, waiting for transfers between devices, inverse_fields(): lax.all_to_all(packed, 'gx', split_axis=3, concat_axis=2, tiled=True)  15.2 us
    all_to_all x1, waiting for transfers between devices, forward(): lax.all_to_all(packed, 'gy', split_axis=3, concat_axis=2, tiled=True)  13.9 us
    squeeze x3, local copies, waits for them, and re-layouts, forward(): pieces[0]  9.63 us
  transfers between devices with their start and end apart: 20, of which 9 were waited for; matrix products, arithmetic and copies ran while one was open for 1% of the time, Pallas kernels for 0%

commit v1 on v0

v1 whole, which is shorter than its diff:
```python
import functools
import math

import jax
import jax.numpy as jnp
import numpy as np
from jax import lax
from jax.experimental import pallas as pl
from jax.experimental.pallas import tpu as pltpu
from jax.sharding import PartitionSpec as P

STEPS = 2
NX, NY, NZ = 512, 256, 128
GX, GY = 64, 8
XL, YL = NX // GX, NY // GY
ROWS = XL * YL
time_step = 0.2

MESH = pl.DeviceIdType.MESH
F32, BF16 = jnp.float32, jnp.bfloat16


def real_form(matrix):
    return np.block([[matrix.real, matrix.imag], [-matrix.imag, matrix.real]])


def left_form(matrix):
    return np.block([[matrix.real, -matrix.imag], [matrix.imag, matrix.real]])


def dft(length, sign):
    k = np.arange(length)
    return np.exp(sign * 2j * math.pi * (np.outer(k, k) % length) / length)


def tables():
    z = np.arange(NZ)
    per = NZ // 2 // GY
    forward_z = np.zeros((NZ, NZ))
    weighted_z = np.zeros((NZ, NZ))
    back_z = np.zeros((NZ, NZ))
    weighted_back = np.zeros((NZ, NZ))
    norm = 1.0 / (NX * NY * NZ)
    for column in range(NZ // 2):
        real_row = (column // per) * 2 * per + column % per
        imag_row = real_row + per
        angle = 2 * math.pi * (column * z % NZ) / NZ
        cosine, sine = np.cos(angle), np.sin(angle)
        if column == 0:
            sign = 1.0 - 2.0 * (z % 2)
            forward_z[real_row], forward_z[imag_row] = 1.0, sign
            back_z[real_row], back_z[imag_row] = norm, norm * sign
        else:
            forward_z[real_row], forward_z[imag_row] = cosine, -sine
            back_z[real_row], back_z[imag_row] = 2 * norm * cosine, -2 * norm * sine
        weighted_z[real_row] = column * forward_z[real_row]
        weighted_z[imag_row] = column * forward_z[imag_row]
        weighted_back[real_row] = column * back_z[real_row]
        weighted_back[imag_row] = column * back_z[imag_row]

    device_y = np.kron(dft(GY, -1), np.eye(per))
    arrive = np.zeros((NZ, NZ))
    for source in range(GY):
        for part in range(2):
            for j in range(per):
                arrive[part * 64 + source * per + j, source * 2 * per + part * per + j] = 1.0
    left_y = left_form(device_y) @ arrive
    left_y_back = arrive.T @ left_form(device_y.conj())
    q1 = np.arange(64) // per
    yl = np.arange(ROWS) % YL
    turn_y = np.exp(-2j * math.pi * (np.outer(q1, yl) % NY) / NY)
    local_y = real_form(np.kron(np.eye(4), dft(YL, -1)))
    local_y_back = real_form(np.kron(np.eye(4), dft(YL, 1)))

    left_x = left_form(dft(GX, -1))
    left_x_back = left_form(dft(GX, 1))
    xl = np.arange(ROWS) // YL
    turn_x = np.exp(-2j * math.pi * (np.outer(np.arange(64), xl) % NX) / NX)
    local_x = []
    for a in range(2):
        small = np.diag(np.exp(-2j * math.pi * a * np.arange(4) / 8)) @ dft(4, -1)
        local_x.append(np.kron(small, np.eye(YL)))
    local_x_back = [real_form(m.conj().T) for m in local_x]
    local_x = [real_form(m) for m in local_x]

    def pair(stack):
        stack = np.stack(stack).astype(np.float32)
        high = stack.astype(BF16)
        low = (stack - high.astype(np.float32)).astype(BF16)
        return np.stack([high, low], axis=1)

    small = pair(
        [forward_z, weighted_z, left_y, left_y_back, left_x, left_x_back, back_z, weighted_back]
    )
    large = pair([local_y, local_y_back] + local_x + local_x_back)
    turns = np.stack([turn_y.real, turn_y.imag, turn_x.real, turn_x.imag]).astype(np.float32)
    return small, large, turns


def split(value):
    high = value.astype(BF16)
    return high, (value - high.astype(F32)).astype(BF16)


def product(left, right, dims):
    def one(a, b):
        return lax.dot_general(a, b, (dims, ((), ())), preferred_element_type=F32)

    return one(left[0], right[0]) + (one(left[0], right[1]) + one(left[1], right[0]))


NN = ((1,), (0,))
NT = ((1,), (1,))
TN = ((0,), (0,))


def matmul(left, right, dims=NN):
    left = left if isinstance(left, tuple) else split(left)
    right = right if isinstance(right, tuple) else split(right)
    return product(left, right, dims)


def turned(real, imag, cosine, sine, back):
    if back:
        return real * cosine + imag * sine, imag * cosine - real * sine
    return real * cosine - imag * sine, imag * cosine + real * sine


def lanes(value, half):
    return value[:, half * 128 : half * 128 + 128]


def z_forward(field, table):
    return matmul(table, field, NT)


def y_forward_left(arrived, left, cosine, sine):
    both = matmul(left, arrived)
    return turned(both[:64], both[64:], cosine, sine, False)


def halves_product(pairs, table):
    stacked = jnp.concatenate(
        [
            jnp.concatenate([lanes(re, h), lanes(im, h)], axis=1)
            for re, im in pairs
            for h in range(2)
        ],
        axis=0,
    )
    out = matmul(stacked, table)
    result = []
    for n in range(len(pairs)):
        rows = [out[(2 * n + h) * 64 : (2 * n + h) * 64 + 64] for h in range(2)]
        result.append(
            tuple(
                jnp.concatenate([r[:, part * 128 : part * 128 + 128] for r in rows], axis=1)
                for part in range(2)
            )
        )
    return result


def signed(positions, length):
    half = length // 2
    value = jnp.where(positions < half, positions, positions - length)
    return jnp.where(positions == half, 0, value).astype(F32)


def iota(axis):
    return lax.broadcasted_iota(jnp.int32, (64, 256), axis)


def wave_y_rows():
    return signed(iota(0) // 8 + 8 * (iota(1) % YL), NY)


def waves_here(gx, gy):
    lane = iota(1)
    k2 = lane // 128 + 2 * (lane % 128 // YL)
    wave_x = signed(iota(0) + 64 * k2, NX)
    wave_y = signed(gx // 8 + 8 * (lane % YL), NY)
    wave_z = (gy * 8 + gx % 8).astype(F32)
    size = wave_x * wave_x + wave_y * wave_y + wave_z * wave_z
    return wave_x, 1.0 / jnp.maximum(size, 1.0)


def x_stage(planes, left, left_back, local, local_back, cosine, sine, wave_x, inverse):
    stacked = jnp.concatenate(
        [
            jnp.concatenate([planes[2 * f][h], planes[2 * f + 1][h]], axis=0)
            for f in range(2)
            for h in range(2)
        ],
        axis=1,
    )
    out = matmul(left, stacked)
    fields = []
    for f in range(2):
        re, im = out[:64, f * 256 : f * 256 + 256], out[64:, f * 256 : f * 256 + 256]
        fields.append(turned(re, im, cosine, sine, False))
    spectra = [[], []]
    for a in range(2):
        rows = []
        for re, im in fields:
            if a == 0:
                re, im = lanes(re, 0) + lanes(re, 1), lanes(im, 0) + lanes(im, 1)
            else:
                re, im = lanes(re, 0) - lanes(re, 1), lanes(im, 0) - lanes(im, 1)
            rows.append(jnp.concatenate([re, im], axis=1))
        got = matmul(jnp.concatenate(rows, axis=0), local[a])
        wave = lanes(wave_x, a)
        scale = lanes(inverse, a)
        phi_re = (wave * got[:64, :128] + got[64:, :128]) * scale
        phi_im = (wave * got[:64, 128:] + got[64:, 128:]) * scale
        both = jnp.concatenate(
            [
                jnp.concatenate([wave * phi_re, wave * phi_im], axis=1),
                jnp.concatenate([phi_re, phi_im], axis=1),
            ],
            axis=0,
        )
        back = matmul(both, local_back[a])
        for f in range(2):
            spectra[a].append((back[f * 64 : f * 64 + 64, :128], back[f * 64 : f * 64 + 64, 128:]))
    stacked = []
    for f in range(2):
        zero, one = spectra[0][f], spectra[1][f]
        for h in range(2):
            if h == 0:
                re, im = zero[0] + one[0], zero[1] + one[1]
            else:
                re, im = zero[0] - one[0], zero[1] - one[1]
            re, im = turned(re, im, lanes(cosine, h), lanes(sine, h), True)
            stacked.append(jnp.concatenate([re, im], axis=0))
    out = matmul(left_back, jnp.concatenate(stacked, axis=1))
    result = []
    for f in range(2):
        for part in range(2):
            rows = out[part * 64 : part * 64 + 64]
            result.append(
                [rows[:, (2 * f + h) * 128 : (2 * f + h) * 128 + 128] for h in range(2)]
            )
    return result


def y_back_left(pair, left, cosine, sine):
    re, im = turned(pair[0], pair[1], cosine, sine, True)
    return matmul(left, jnp.concatenate([re, im], axis=0))


def z_back(arrived, table):
    return matmul(arrived, table, TN)


def kernel(
    velocity, stress, lame, shear, buoy, source_p, source_s, small, large, turns,
    image_p, image_s,
    v_0, v_1, v_2, s_0, s_1, s_2, lame_v, shear_v, buoy_v, source_p_v, source_s_v,
    small_v, large_v, turns_v, y_send, y_recv,
    z_send, z_recv, x_send, x_recv, x_send_2, x_recv_2, z_send_2, z_recv_2,
    load_sem, own_sem, halo_send, halo_recv, gy_send, gy_recv, gx_send, gx_recv,
):
    gx, gy = lax.axis_index("gx"), lax.axis_index("gy")

    def interior(ref):
        return ref.at[:, pl.ds(YL, ROWS)]

    loads = [
        (velocity, interior(v_0)),
        (stress, s_0),
        (lame, lame_v),
        (shear, shear_v),
        (buoy, buoy_v),
        (small, small_v),
        (large, large_v),
        (turns, turns_v),
        (source_p, source_p_v),
        (source_s, source_s_v),
    ]
    loads = [pltpu.make_async_copy(a, b, load_sem.at[n]) for n, (a, b) in enumerate(loads)]
    for load in loads:
        load.start()

    barrier = pltpu.get_barrier_semaphore()

    def greet_x(k, carry):
        pl.semaphore_signal(
            barrier, inc=1, device_id=(lax.rem(gx + k, GX), gy), device_id_type=MESH
        )
        return carry

    def greet_y(k, carry):
        pl.semaphore_signal(
            barrier, inc=1, device_id=(gx, lax.rem(gy + k, GY)), device_id_type=MESH
        )
        return carry

    lax.fori_loop(1, GX, greet_x, 0)
    lax.fori_loop(1, GY, greet_y, 0)
    pl.semaphore_wait(barrier, GX + GY - 2)

    right_x, left_x = (lax.rem(gx + 1, GX), gy), (lax.rem(gx + GX - 1, GX), gy)
    right_y, left_y = (gx, lax.rem(gy + 1, GY)), (gx, lax.rem(gy + GY - 1, GY))

    def send(source, target, device, send_sem, recv_sem):
        copy = pltpu.make_async_remote_copy(
            src_ref=source,
            dst_ref=target,
            send_sem=send_sem,
            recv_sem=recv_sem,
            device_id=device,
            device_id_type=MESH,
        )
        copy.start()
        return copy

    first, last = pl.ds(YL, YL), pl.ds(ROWS, YL)
    below, above = pl.ds(0, YL), pl.ds(ROWS + YL, YL)
    top_rows = pl.ds(YL, XL, stride=YL)
    end_rows = pl.ds(2 * YL - 1, XL, stride=YL)

    def exchange(ref, turn, x_prior, x_next, y_prior, y_next):
        slot = 0
        for field in y_prior:
            y_send[turn, slot] = ref[field, end_rows, :]
            slot += 1
        for field in y_next:
            y_send[turn, slot] = ref[field, top_rows, :]
            slot += 1
        low, high = pl.ds(0, len(y_prior)), pl.ds(len(y_prior), len(y_next))
        a, b = pl.ds(*x_prior), pl.ds(*x_next)
        plan = [
            (y_send.at[turn, low], y_recv.at[turn, low], right_y),
            (y_send.at[turn, high], y_recv.at[turn, high], left_y),
            (ref.at[a, last], ref.at[a, below], right_x),
            (ref.at[b, first], ref.at[b, above], left_x),
        ]
        copies = [
            send(source, target, device, halo_send.at[turn, n], halo_recv.at[turn, n])
            for n, (source, target, device) in enumerate(plan)
        ]
        for copy in copies:
            copy.wait()

        @pl.when(gx == 0)
        def _():
            for n in range(x_prior[1]):
                ref[x_prior[0] + n, below, :] = jnp.zeros((YL, NZ), F32)

        @pl.when(gx == GX - 1)
        def _():
            for n in range(x_next[1]):
                ref[x_next[0] + n, above, :] = jnp.zeros((YL, NZ), F32)

        @pl.when(gy == 0)
        def _():
            for n in range(len(y_prior)):
                y_recv[turn, n] = jnp.zeros((XL, NZ), F32)

        @pl.when(gy == GY - 1)
        def _():
            for n in range(len(y_next)):
                y_recv[turn, len(y_prior) + n] = jnp.zeros((XL, NZ), F32)

    z_lane = lax.broadcasted_iota(jnp.int32, (YL, NZ), 1)
    y_row = lax.broadcasted_iota(jnp.int32, (YL, NZ), 0)

    def next_z(f):
        return jnp.where(z_lane == NZ - 1, 0.0, pltpu.roll(f, NZ - 1, 1))

    def prior_z(f):
        return jnp.where(z_lane == 0, 0.0, pltpu.roll(f, 1, 1))

    def next_y(f, rim):
        return jnp.where(y_row == YL - 1, rim, pltpu.roll(f, YL - 1, 0))

    def prior_y(f, rim):
        return jnp.where(y_row == 0, rim, pltpu.roll(f, 1, 0))

    def stress_update(v, s_in, s_in_base, s_out, turn):
        def plane(i, carry):
            here = pl.ds(pl.multiple_of((i + 1) * YL, YL), YL)
            before = pl.ds(pl.multiple_of(i * YL, YL), YL)
            after = pl.ds(pl.multiple_of((i + 2) * YL, YL), YL)
            inner = pl.ds(pl.multiple_of(i * YL, YL), YL)
            old = pl.ds(pl.multiple_of(i * YL + s_in_base, YL), YL)

            def rim(n):
                return y_recv[turn, n, pl.ds(i, 1), :]

            v_x, v_y, v_z = v[0, here, :], v[1, here, :], v[2, here, :]
            lam = lame_v[inner, :].astype(F32) * time_step
            mu = shear_v[inner, :].astype(F32) * time_step
            e_x = v_x - v[0, before, :]
            e_y = v_y - prior_y(v_y, rim(0))
            e_z = v_z - prior_z(v_z)
            volume = lam * (e_x + e_y + e_z)
            twice = 2.0 * mu
            s_out[0, here, :] = s_in[0, old, :] + (volume + twice * e_x)
            s_out[1, here, :] = s_in[1, old, :] + (volume + twice * e_y)
            s_out[2, here, :] = s_in[2, old, :] + (volume + twice * e_z)
            s_out[3, here, :] = s_in[3, old, :] + mu * (
                (next_y(v_x, rim(1)) - v_x) + (v[1, after, :] - v_y)
            )
            s_out[4, here, :] = s_in[4, old, :] + mu * (
                (next_z(v_x) - v_x) + (v[2, after, :] - v_z)
            )
            s_out[5, here, :] = s_in[5, old, :] + mu * (
                (next_z(v_y) - v_y) + (next_y(v_z, rim(2)) - v_z)
            )
            return carry

        lax.fori_loop(0, XL, plane, 0)

    def velocity_update(v_in, s, v_out, turn):
        def plane(i, carry):
            here = pl.ds(pl.multiple_of((i + 1) * YL, YL), YL)
            before = pl.ds(pl.multiple_of(i * YL, YL), YL)
            after = pl.ds(pl.multiple_of((i + 2) * YL, YL), YL)
            inner = pl.ds(pl.multiple_of(i * YL, YL), YL)

            def rim(n):
                return y_recv[turn, n, pl.ds(i, 1), :]

            b = buoy_v[inner, :].astype(F32) * time_step
            xx, yy, zz = s[0, here, :], s[1, here, :], s[2, here, :]
            xy, xz, yz = s[3, here, :], s[4, here, :], s[5, here, :]
            v_out[0, here, :] = v_in[0, here, :] + b * (
                (s[0, after, :] - xx) + (xy - prior_y(xy, rim(0))) + (xz - prior_z(xz))
            )
            v_out[1, here, :] = v_in[1, here, :] + b * (
                (xy - s[3, before, :]) + (next_y(yy, rim(2)) - yy) + (yz - prior_z(yz))
            )
            v_out[2, here, :] = v_in[2, here, :] + b * (
                (xz - s[4, before, :]) + (yz - prior_y(yz, rim(1))) + (next_z(zz) - zz)
            )
            return carry

        lax.fori_loop(0, XL, plane, 0)

    loads[0].wait()
    exchange(v_0, 0, (0, 1), (1, 2), [1], [0, 2])
    for load in loads[1:4]:
        load.wait()
    stress_update(v_0, s_0, 0, s_1, 0)
    exchange(s_1, 1, (3, 2), (0, 1), [3, 5], [1])
    loads[4].wait()
    velocity_update(v_0, s_1, v_1, 1)
    exchange(v_1, 2, (0, 1), (1, 2), [1], [0, 2])
    stress_update(v_1, s_1, YL, s_2, 2)
    exchange(s_2, 3, (3, 2), (0, 1), [3, 5], [1])
    velocity_update(v_1, s_2, v_2, 3)

    for load in loads[5:8]:
        load.wait()

    def narrow(n):
        return small_v[n, 0], small_v[n, 1]

    def wide(n):
        return large_v[n, 0], large_v[n, 1]

    def all_to_all_gy(field, sent, received, turn):
        mine = pl.ds(pl.multiple_of(gy * 16, 16), 16)

        def one(k, carry):
            to = lax.rem(gy + k, GY)
            send(
                sent.at[field, pl.ds(pl.multiple_of(to * 16, 16), 16)],
                received.at[field, mine],
                (gx, to),
                gy_send.at[turn, field],
                gy_recv.at[turn, field],
            )
            return carry

        lax.fori_loop(1, GY, one, 0)
        received[field, mine, :] = sent[field, mine, :]

    def wait_gy(field, received, sems, turn):
        part = received.at[field, pl.ds(0, 16 * (GY - 1))]
        pltpu.make_async_copy(part, part, sems.at[turn, field]).wait()

    def all_to_all_gx(sent, received, turn):
        mine = pl.ds(pl.multiple_of(gx * 8, 8), 8)

        def one(k, carry):
            to = lax.rem(gx + k, GX)
            send(
                sent.at[pl.ds(pl.multiple_of(to * 8, 8), 8)],
                received.at[mine],
                (to, gy),
                gx_send.at[turn],
                gx_recv.at[turn],
            )
            return carry

        lax.fori_loop(1, GX, one, 0)
        received[mine, :] = sent[mine, :]

    def wait_gx(received, sems, turn):
        part = received.at[pl.ds(0, 8 * (GX - 1))]
        pltpu.make_async_copy(part, part, sems.at[turn]).wait()

    turn_y = turns_v[0], turns_v[1]
    turn_x = turns_v[2], turns_v[3]

    for field in range(3):
        table = narrow(1 if field == 2 else 0)
        z_send[field] = z_forward(v_2[field, pl.ds(YL, ROWS), :], table)
        all_to_all_gy(field, z_send, z_recv, 0)

    pairs = []
    for field in range(3):
        wait_gy(field, z_recv, gy_recv, 0)
        pairs.append(y_forward_left(z_recv[field], narrow(2), *turn_y))
    pairs = halves_product(pairs, wide(0))
    wave_y = wave_y_rows()
    joined = [wave_y * pairs[1][part] + pairs[2][part] for part in range(2)]
    for p, value in enumerate([pairs[0][0], pairs[0][1]] + joined):
        for h in range(2):
            x_send[pl.ds(2 * p + h, 64, stride=8), :] = lanes(value, h)
    all_to_all_gx(x_send, x_recv, 0)

    wave_x, inverse = waves_here(gx, gy)
    wait_gx(x_recv, gx_recv, 0)
    planes = [[x_recv[pl.ds(2 * p + h, 64, stride=8), :] for h in range(2)] for p in range(4)]
    planes = x_stage(
        planes,
        narrow(4),
        narrow(5),
        [wide(2), wide(3)],
        [wide(4), wide(5)],
        *turn_x,
        wave_x,
        inverse,
    )
    for p in range(4):
        for h in range(2):
            x_send_2[pl.ds(2 * p + h, 64, stride=8), :] = planes[p][h]
    all_to_all_gx(x_send_2, x_recv_2, 1)

    wait_gx(x_recv_2, gx_recv, 1)
    planes = [
        jnp.concatenate([x_recv_2[pl.ds(2 * p + h, 64, stride=8), :] for h in range(2)], axis=1)
        for p in range(4)
    ]
    pairs = [
        (planes[0], planes[1]),
        (wave_y * planes[2], wave_y * planes[3]),
        (planes[2], planes[3]),
    ]
    pairs = halves_product(pairs, wide(1))
    for field in range(3):
        z_send_2[field] = y_back_left(pairs[field], narrow(3), *turn_y)
        all_to_all_gy(field, z_send_2, z_recv_2, 1)

    for load in loads[8:]:
        load.wait()
    total_p = jnp.zeros((ROWS, NZ), F32)
    total_s = jnp.zeros((ROWS, NZ), F32)
    for field in range(3):
        wait_gy(field, z_recv_2, gy_recv, 1)
        p_field = z_back(z_recv_2[field], narrow(7 if field == 2 else 6))
        s_field = v_2[field, pl.ds(YL, ROWS), :] - p_field
        total_p += source_p_v[field].astype(F32) * p_field
        total_s += source_s_v[field].astype(F32) * s_field
    image_p[...] = total_p
    image_s[...] = total_s

    for field in range(3):
        wait_gy(field, z_send, gy_send, 0)
        wait_gy(field, z_send_2, gy_send, 1)
    wait_gx(x_send, gx_send, 0)
    wait_gx(x_send_2, gx_send, 1)


def shards(small, large, turns, velocity, stress, lame, shear, buoy, source_p, source_s):
    any_space = pl.BlockSpec(memory_space=pl.ANY)
    padded = (XL + 2) * YL
    dma = pltpu.SemaphoreType.DMA
    scratch = [
        *[pltpu.VMEM((3, padded, NZ), F32)] * 3,
        pltpu.VMEM((6, ROWS, NZ), F32),
        *[pltpu.VMEM((6, padded, NZ), F32)] * 2,
        *[pltpu.VMEM((ROWS, NZ), BF16)] * 3,
        *[pltpu.VMEM((3, ROWS, NZ), BF16)] * 2,
        pltpu.VMEM(small.shape, BF16),
        pltpu.VMEM(large.shape, BF16),
        pltpu.VMEM(turns.shape, F32),
        *[pltpu.VMEM((4, 3, XL, NZ), F32)] * 2,
        *[pltpu.VMEM((3, NZ, ROWS), F32)] * 2,
        *[pltpu.VMEM((8 * GX, NZ), F32)] * 4,
        *[pltpu.VMEM((3, NZ, ROWS), F32)] * 2,
        dma((10,)),
        dma((1,)),
        dma((4, 4)),
        dma((4, 4)),
        dma((2, 3)),
        dma((2, 3)),
        dma((2,)),
        dma((2,)),
    ]
    out = jax.ShapeDtypeStruct((ROWS, NZ), F32)
    outs = pl.pallas_call(
        kernel,
        out_shape=(out, out),
        in_specs=[any_space] * 10,
        out_specs=(pl.BlockSpec(memory_space=pltpu.VMEM),) * 2,
        scratch_shapes=scratch,
        compiler_params=pltpu.CompilerParams(
            collective_id=0, has_side_effects=True, vmem_limit_bytes=40 * 2**20
        ),
    )(
        velocity.reshape(3, ROWS, NZ),
        stress.reshape(6, ROWS, NZ),
        lame.reshape(ROWS, NZ),
        shear.reshape(ROWS, NZ),
        buoy.reshape(ROWS, NZ),
        source_p.reshape(3, ROWS, NZ),
        source_s.reshape(3, ROWS, NZ),
        small,
        large,
        turns,
    )
    return tuple(o.reshape(XL, YL, NZ) for o in outs)


def solution(mesh):
    small, large, turns = tables()

    def body(*blocks):
        return shards(jnp.asarray(small), jnp.asarray(large), jnp.asarray(turns), *blocks)

    in_specs = (
        P(None, "gx", "gy", None),
        P(None, "gx", "gy", None),
        P("gx", "gy", None),
        P("gx", "gy", None),
        P("gx", "gy", None),
        P(None, "gx", "gy", None),
        P(None, "gx", "gy", None),
    )
    out_specs = (P("gx", "gy", None), P("gx", "gy", None))
    return jax.shard_map(body, mesh=mesh, in_specs=in_specs, out_specs=out_specs, check_vma=False)
```

time: 327 us -> 99.6 us (0.30)
  the two profiles are of different devices: /device:TPU:64 before, /device:TPU:1 now
where the time goes in v1:
time: 99.6 us; the launch traced here: 98.5 us
  Pallas kernels  86.6 us (87%)
  local copies, waits for them, and re-layouts  11.2 us (11%)
    pallas_call x1, Pallas kernels, shards(): pl.pallas_call(kernel, out_shape=(out, out), in_specs=[any_space] * 10, o...  86.6 us
    unnamed x22, local copies, waits for them, and re-layouts  11.2 us

profile of v1, /device:TPU:1, one launch (start us, length us, event | category | flops | bytes accessed | tf_op | source)
XLA Modules:
  0.0 98.5 jit_solution(16161259636507830597)
XLA Ops:
  0.6 0.0 copy-start
  0.6 1.4 %copy-done = bf16[6,2,256,256]{3,2,1,0:T(8,128)(2,1)S(1)} copy-done((bf16[6,2,256,256]{3,2,1,0:T(8,128)(2,1)S(1)}, bf16[6,2,256,256]{3,2,1,0:T(8,128)(2,1)}, u32[]{:S(2)}) %copy-start) | copy-done | bytes 1572888
  2.0 0.0 copy-start.1
  2.0 1.1 %copy-done.1 = f32[6,8,32,128]{3,2,1,0:T(8,128)S(1)} copy-done((f32[6,8,32,128]{3,2,1,0:T(8,128)S(1)}, f32[6,8,32,128]{3,2,1,0:T(8,128)}, u32[]{:S(2)}) %copy-start.1) | copy-done | bytes 786456
  3.2 0.0 copy-start.2
  3.2 1.0 %copy-done.2 = bf16[8,2,128,128]{3,2,1,0:T(8,128)(2,1)S(1)} copy-done((bf16[8,2,128,128]{3,2,1,0:T(8,128)(2,1)S(1)}, bf16[8,2,128,128]{3,2,1,0:T(8,128)(2,1)}, u32[]{:S(2)}) %copy-start.2) | copy-done | bytes 524312
  4.2 0.0 copy-start.3
  4.2 1.0 %copy-done.3 = f32[3,8,32,128]{3,2,1,0:T(8,128)S(1)} copy-done((f32[3,8,32,128]{3,2,1,0:T(8,128)S(1)}, f32[3,8,32,128]{3,2,1,0:T(8,128)}, u32[]{:S(2)}) %copy-start.3) | copy-done | bytes 393240
  5.2 0.0 copy-start.4
  5.2 0.9 copy-done.4
  6.2 0.0 copy-start.5
  6.2 0.9 copy-done.5
  7.1 0.0 copy-start.6
  7.1 0.9 copy-done.6
  8.0 0.0 copy-start.7
  8.0 0.8 copy-done.7
  8.9 0.0 copy-start.8
  8.9 0.8 copy-done.8
  9.7 0.0 copy-start.9
  9.7 0.8 copy-done.9
  10.5 86.6 %shard_map.113 = (f32[256,128]{1,0:T(8,128)S(1)}, f32[256,128]{1,0:T(8,128)S(1)}) custom-call(f32[3,256,128]{2,1,0:T(8,128)S(1)} %bitcast.10, f32[6,256,128]{2,1,0:T(8,128)S(1)} %bitcast.9, bf16[256,128]{1,0:T(8,128)(2,1)S(1)} %bitcast.15, bf16[256,128]{1,0:T(8,128)(2,1)S(1)} %bitcast.16, bf16[256,128]{1,0:T(8,128)(2,1)S(1)} %bitcast.17, ...), custom_call_target="tpu_custom_call" | custom-call | tf_op jit(solution)/shard_map/pallas_call | solution.py:606
  97.2 0.7 copy.14
  97.8 0.7 copy.15
Async XLA Ops:
  0.6 1.4 %copy-start = (bf16[6,2,256,256]{3,2,1,0:T(8,128)(2,1)S(1)}, bf16[6,2,256,256]{3,2,1,0:T(8,128)(2,1)}, u32[]{:S(2)}) copy-start(bf16[6,2,256,256]{3,2,1,0:T(8,128)(2,1)} %constant.7.clone.large) | copy-start | bytes 4718596
  2.0 1.1 %copy-start.1 = (f32[6,8,32,128]{3,2,1,0:T(8,128)S(1)}, f32[6,8,32,128]{3,2,1,0:T(8,128)}, u32[]{:S(2)}) copy-start(f32[6,8,32,128]{3,2,1,0:T(8,128)} %param.11) | copy-start | bytes 2359300
  3.2 1.0 %copy-start.2 = (bf16[8,2,128,128]{3,2,1,0:T(8,128)(2,1)S(1)}, bf16[8,2,128,128]{3,2,1,0:T(8,128)(2,1)}, u32[]{:S(2)}) copy-start(bf16[8,2,128,128]{3,2,1,0:T(8,128)(2,1)} %constant.6.clone.small) | copy-start | bytes 1572868
  4.2 1.0 %copy-start.3 = (f32[3,8,32,128]{3,2,1,0:T(8,128)S(1)}, f32[3,8,32,128]{3,2,1,0:T(8,128)}, u32[]{:S(2)}) copy-start(f32[3,8,32,128]{3,2,1,0:T(8,128)} %param.10) | copy-start | bytes 1179652
  5.2 0.9 copy-start.4
  6.2 0.9 copy-start.5
  7.1 0.9 copy-start.6
  8.0 0.8 copy-start.7
  8.9 0.8 copy-start.8
  9.7 0.8 copy-start.9

commit v2 on v1

--- a/solution.py
+++ b/solution.py
@@ -256,21 +256,41 @@
 def kernel(
     velocity, stress, lame, shear, buoy, source_p, source_s, small, large, turns,
     image_p, image_s,
-    v_0, v_1, v_2, s_0, s_1, s_2, lame_v, shear_v, buoy_v, source_p_v, source_s_v,
-    small_v, large_v, turns_v, y_send, y_recv,
+    v_0, v_1, v_2, s_0, s_1, rims, lame_v, shear_v, buoy_v, source_p_v, source_s_v,
+    small_v, large_v, turns_v, moduli, y_send, y_recv, y_send_2, y_recv_2, corners,
     z_send, z_recv, x_send, x_recv, x_send_2, x_recv_2, z_send_2, z_recv_2,
-    load_sem, own_sem, halo_send, halo_recv, gy_send, gy_recv, gx_send, gx_recv,
+    load_sem, halo_send, halo_recv, gy_send, gy_recv, gx_send, gx_recv,
 ):
     gx, gy = lax.axis_index("gx"), lax.axis_index("gy")
 
+    barrier = pltpu.get_barrier_semaphore()
+
+    def greet(device):
+        pl.semaphore_signal(barrier, inc=1, device_id=device, device_id_type=MESH)
+
+    def greet_x(k, carry):
+        greet((lax.rem(gx + k, GX), gy))
+        return carry
+
+    def greet_y(k, carry):
+        greet((gx, lax.rem(gy + k, GY)))
+        return carry
+
+    next_gx, prior_gx = lax.rem(gx + 1, GX), lax.rem(gx + GX - 1, GX)
+    next_gy, prior_gy = lax.rem(gy + 1, GY), lax.rem(gy + GY - 1, GY)
+    greet((next_gx, prior_gy))
+    greet((prior_gx, next_gy))
+    lax.fori_loop(1, GY, greet_y, 0)
+    lax.fori_loop(1, GX, greet_x, 0)
+
     def interior(ref):
         return ref.at[:, pl.ds(YL, ROWS)]
 
     loads = [
-        (velocity, interior(v_0)),
-        (stress, s_0),
         (lame, lame_v),
         (shear, shear_v),
+        (velocity, interior(v_0)),
+        (stress, interior(s_0)),
         (buoy, buoy_v),
         (small, small_v),
         (large, large_v),
@@ -281,27 +301,6 @@
     loads = [pltpu.make_async_copy(a, b, load_sem.at[n]) for n, (a, b) in enumerate(loads)]
     for load in loads:
         load.start()
-
-    barrier = pltpu.get_barrier_semaphore()
-
-    def greet_x(k, carry):
-        pl.semaphore_signal(
-            barrier, inc=1, device_id=(lax.rem(gx + k, GX), gy), device_id_type=MESH
-        )
-        return carry
-
-    def greet_y(k, carry):
-        pl.semaphore_signal(
-            barrier, inc=1, device_id=(gx, lax.rem(gy + k, GY)), device_id_type=MESH
-        )
-        return carry
-
-    lax.fori_loop(1, GX, greet_x, 0)
-    lax.fori_loop(1, GY, greet_y, 0)
-    pl.semaphore_wait(barrier, GX + GY - 2)
-
-    right_x, left_x = (lax.rem(gx + 1, GX), gy), (lax.rem(gx + GX - 1, GX), gy)
-    right_y, left_y = (gx, lax.rem(gy + 1, GY)), (gx, lax.rem(gy + GY - 1, GY))
 
     def send(source, target, device, send_sem, recv_sem):
         copy = pltpu.make_async_remote_copy(
@@ -319,138 +318,241 @@
     below, above = pl.ds(0, YL), pl.ds(ROWS + YL, YL)
     top_rows = pl.ds(YL, XL, stride=YL)
     end_rows = pl.ds(2 * YL - 1, XL, stride=YL)
-
-    def exchange(ref, turn, x_prior, x_next, y_prior, y_next):
-        slot = 0
-        for field in y_prior:
-            y_send[turn, slot] = ref[field, end_rows, :]
-            slot += 1
-        for field in y_next:
-            y_send[turn, slot] = ref[field, top_rows, :]
-            slot += 1
-        low, high = pl.ds(0, len(y_prior)), pl.ds(len(y_prior), len(y_next))
-        a, b = pl.ds(*x_prior), pl.ds(*x_next)
+    every = pl.ds(0, 3)
+    sent = []
+
+    def exchange(turn, v, sending, receiving, more):
         plan = [
-            (y_send.at[turn, low], y_recv.at[turn, low], right_y),
-            (y_send.at[turn, high], y_recv.at[turn, high], left_y),
-            (ref.at[a, last], ref.at[a, below], right_x),
-            (ref.at[b, first], ref.at[b, above], left_x),
-        ]
+            (sending.at[0], receiving.at[0], (gx, next_gy)),
+            (sending.at[1], receiving.at[1], (gx, prior_gy)),
+            (sending.at[0, 1], corners.at[turn, 0], (prior_gx, next_gy)),
+            (sending.at[1, 0], corners.at[turn, 1], (next_gx, prior_gy)),
+            (v.at[every, last], v.at[every, below], (next_gx, gy)),
+            (v.at[every, first], v.at[every, above], (prior_gx, gy)),
+        ] + more
         copies = [
             send(source, target, device, halo_send.at[turn, n], halo_recv.at[turn, n])
             for n, (source, target, device) in enumerate(plan)
         ]
+        sent.extend(copies)
+        return copies
+
+    def arrive(turn, copies, v, receiving, fields):
         for copy in copies:
-            copy.wait()
+            copy.wait_recv()
+        nothing = jnp.zeros((YL, NZ), F32)
 
         @pl.when(gx == 0)
         def _():
-            for n in range(x_prior[1]):
-                ref[x_prior[0] + n, below, :] = jnp.zeros((YL, NZ), F32)
+            for n in range(3):
+                v[n, below, :] = nothing
+            if turn == 0:
+                s_0[3, below, :] = nothing
+                s_0[4, below, :] = nothing
+                moduli[1, below, :] = nothing
+            corners[turn, 1] = nothing[:XL]
 
         @pl.when(gx == GX - 1)
         def _():
-            for n in range(x_next[1]):
-                ref[x_next[0] + n, above, :] = jnp.zeros((YL, NZ), F32)
+            for n in range(3):
+                v[n, above, :] = nothing
+            if turn == 0:
+                s_0[0, above, :] = nothing
+                moduli[0, above, :] = nothing
+                moduli[1, above, :] = nothing
+            corners[turn, 0] = nothing[:XL]
 
         @pl.when(gy == 0)
         def _():
-            for n in range(len(y_prior)):
-                y_recv[turn, n] = jnp.zeros((XL, NZ), F32)
+            for n in range(fields):
+                receiving[0, n] = nothing[:XL]
+            corners[turn, 0] = nothing[:XL]
 
         @pl.when(gy == GY - 1)
         def _():
-            for n in range(len(y_next)):
-                y_recv[turn, len(y_prior) + n] = jnp.zeros((XL, NZ), F32)
-
-    z_lane = lax.broadcasted_iota(jnp.int32, (YL, NZ), 1)
-    y_row = lax.broadcasted_iota(jnp.int32, (YL, NZ), 0)
+            for n in range(fields):
+                receiving[1, n] = nothing[:XL]
+            corners[turn, 1] = nothing[:XL]
+
+    def at_row(f, row):
+        return lax.broadcasted_iota(jnp.int32, f.shape, 0) == row
+
+    def at_lane(f, lane):
+        return lax.broadcasted_iota(jnp.int32, f.shape, 1) == lane
 
     def next_z(f):
-        return jnp.where(z_lane == NZ - 1, 0.0, pltpu.roll(f, NZ - 1, 1))
+        return jnp.where(at_lane(f, NZ - 1), 0.0, pltpu.roll(f, NZ - 1, 1))
 
     def prior_z(f):
-        return jnp.where(z_lane == 0, 0.0, pltpu.roll(f, 1, 1))
-
-    def next_y(f, rim):
-        return jnp.where(y_row == YL - 1, rim, pltpu.roll(f, YL - 1, 0))
-
-    def prior_y(f, rim):
-        return jnp.where(y_row == 0, rim, pltpu.roll(f, 1, 0))
-
-    def stress_update(v, s_in, s_in_base, s_out, turn):
+        return jnp.where(at_lane(f, 0), 0.0, pltpu.roll(f, 1, 1))
+
+    def next_row(f, rim):
+        return jnp.where(at_row(f, f.shape[0] - 1), rim, pltpu.roll(f, f.shape[0] - 1, 0))
+
+    def prior_row(f, rim):
+        return jnp.where(at_row(f, 0), rim, pltpu.roll(f, 1, 0))
+
+    def plane_at(i):
+        return i if isinstance(i, int) else pl.multiple_of(i, YL)
+
+    def over_planes(plane):
+        plane(0, False, True)
+
+        def middle(i, carry):
+            plane(i, True, True)
+            return carry
+
+        lax.fori_loop(1, XL - 1, middle, 0)
+        plane(XL - 1, True, False)
+
+    def stress_inside(v, s_in, s_out):
+        def plane(i, has_before, has_after):
+            here = pl.ds(plane_at((i + 1) * YL), YL)
+            before = pl.ds(plane_at(i * YL), YL)
+            after = pl.ds(plane_at((i + 2) * YL), YL)
+            v_x, v_y, v_z = v[0, here, :], v[1, here, :], v[2, here, :]
+            lam, mu = moduli[0, here, :], moduli[1, here, :]
+            e_x = v_x - v[0, before, :] if has_before else v_x
+            e_y = v_y - prior_row(v_y, 0.0)
+            e_z = v_z - prior_z(v_z)
+            x_y = v[1, after, :] - v_y if has_after else -v_y
+            x_z = v[2, after, :] - v_z if has_after else -v_z
+            volume = lam * (e_x + e_y + e_z)
+            twice = 2.0 * mu
+            s_out[0, here, :] = s_in[0, here, :] + (volume + twice * e_x)
+            s_out[1, here, :] = s_in[1, here, :] + (volume + twice * e_y)
+            s_out[2, here, :] = s_in[2, here, :] + (volume + twice * e_z)
+            s_out[3, here, :] = s_in[3, here, :] + mu * ((next_row(v_x, 0.0) - v_x) + x_y)
+            s_out[4, here, :] = s_in[4, here, :] + mu * ((next_z(v_x) - v_x) + x_z)
+            s_out[5, here, :] = s_in[5, here, :] + mu * (
+                (next_z(v_y) - v_y) + (next_row(v_z, 0.0) - v_z)
+            )
+
+        over_planes(plane)
+
+    def stress_rims(v, s_in, s_out, received, turn):
+        prior_side = [received[0, n] for n in range(3)]
+        next_side = [received[1, n] for n in range(3)]
+        corner_y = corners[turn, 0, pl.ds(0, 1), :]
+        corner_x = corners[turn, 1, pl.ds(XL - 1, 1), :]
+
+        gone = v[0, below, :]
+        lam, mu = moduli[0, first, :], moduli[1, first, :]
+        s_out[0, first, :] -= (lam + 2.0 * mu) * gone
+        s_out[1, first, :] -= lam * gone
+        s_out[2, first, :] -= lam * gone
+        mu = moduli[1, last, :]
+        s_out[3, last, :] += mu * v[1, above, :]
+        s_out[4, last, :] += mu * v[2, above, :]
+
+        gone = prior_side[1]
+        lam, mu = moduli[0, top_rows, :], moduli[1, top_rows, :]
+        s_out[0, top_rows, :] -= lam * gone
+        s_out[1, top_rows, :] -= (lam + 2.0 * mu) * gone
+        s_out[2, top_rows, :] -= lam * gone
+        mu = moduli[1, end_rows, :]
+        s_out[3, end_rows, :] += mu * next_side[0]
+        s_out[5, end_rows, :] += mu * next_side[2]
+
+        v_x, v_y, v_z = v[0, above, :], v[1, above, :], v[2, above, :]
+        lam, mu = moduli[0, above, :], moduli[1, above, :]
+        e_x = v_x - v[0, last, :]
+        e_y = v_y - prior_row(v_y, corner_y)
+        e_z = v_z - prior_z(v_z)
+        s_out[0, above, :] = s_in[0, above, :] + (lam * (e_x + e_y + e_z) + 2.0 * mu * e_x)
+
+        v_x, v_y, v_z = v[0, below, :], v[1, below, :], v[2, below, :]
+        mu = moduli[1, below, :]
+        s_out[3, below, :] = s_in[3, below, :] + mu * (
+            (next_row(v_x, corner_x) - v_x) + (v[1, first, :] - v_y)
+        )
+        s_out[4, below, :] = s_in[4, below, :] + mu * (
+            (next_z(v_x) - v_x) + (v[2, first, :] - v_z)
+        )
+
+        v_x, v_y, v_z = next_side
+        lam, mu = y_recv[1, 4], y_recv[1, 5]
+        e_x = v_x - prior_row(v_x, corner_x)
+        e_y = v_y - v[1, end_rows, :]
+        e_z = v_z - prior_z(v_z)
+        old = y_recv[1, 3] if turn == 0 else rims[0]
+        rims[0] = old + (lam * (e_x + e_y + e_z) + 2.0 * mu * e_y)
+
+        v_x, v_y, v_z = prior_side
+        mu = y_recv[0, 5]
+        old = y_recv[0, 3] if turn == 0 else rims[1]
+        rims[1] = old + mu * ((v[0, top_rows, :] - v_x) + (next_row(v_y, corner_y) - v_y))
+        old = y_recv[0, 4] if turn == 0 else rims[2]
+        rims[2] = old + mu * ((next_z(v_y) - v_y) + (v[2, top_rows, :] - v_z))
+
+    def velocity_update(v_in, s, v_out):
         def plane(i, carry):
             here = pl.ds(pl.multiple_of((i + 1) * YL, YL), YL)
             before = pl.ds(pl.multiple_of(i * YL, YL), YL)
             after = pl.ds(pl.multiple_of((i + 2) * YL, YL), YL)
             inner = pl.ds(pl.multiple_of(i * YL, YL), YL)
-            old = pl.ds(pl.multiple_of(i * YL + s_in_base, YL), YL)
 
             def rim(n):
-                return y_recv[turn, n, pl.ds(i, 1), :]
-
-            v_x, v_y, v_z = v[0, here, :], v[1, here, :], v[2, here, :]
-            lam = lame_v[inner, :].astype(F32) * time_step
-            mu = shear_v[inner, :].astype(F32) * time_step
-            e_x = v_x - v[0, before, :]
-            e_y = v_y - prior_y(v_y, rim(0))
-            e_z = v_z - prior_z(v_z)
-            volume = lam * (e_x + e_y + e_z)
-            twice = 2.0 * mu
-            s_out[0, here, :] = s_in[0, old, :] + (volume + twice * e_x)
-            s_out[1, here, :] = s_in[1, old, :] + (volume + twice * e_y)
-            s_out[2, here, :] = s_in[2, old, :] + (volume + twice * e_z)
-            s_out[3, here, :] = s_in[3, old, :] + mu * (
-                (next_y(v_x, rim(1)) - v_x) + (v[1, after, :] - v_y)
-            )
-            s_out[4, here, :] = s_in[4, old, :] + mu * (
-                (next_z(v_x) - v_x) + (v[2, after, :] - v_z)
-            )
-            s_out[5, here, :] = s_in[5, old, :] + mu * (
-                (next_z(v_y) - v_y) + (next_y(v_z, rim(2)) - v_z)
-            )
-            return carry
-
-        lax.fori_loop(0, XL, plane, 0)
-
-    def velocity_update(v_in, s, v_out, turn):
-        def plane(i, carry):
-            here = pl.ds(pl.multiple_of((i + 1) * YL, YL), YL)
-            before = pl.ds(pl.multiple_of(i * YL, YL), YL)
-            after = pl.ds(pl.multiple_of((i + 2) * YL, YL), YL)
-            inner = pl.ds(pl.multiple_of(i * YL, YL), YL)
-
-            def rim(n):
-                return y_recv[turn, n, pl.ds(i, 1), :]
+                return rims[n, pl.ds(i, 1), :]
 
             b = buoy_v[inner, :].astype(F32) * time_step
             xx, yy, zz = s[0, here, :], s[1, here, :], s[2, here, :]
             xy, xz, yz = s[3, here, :], s[4, here, :], s[5, here, :]
             v_out[0, here, :] = v_in[0, here, :] + b * (
-                (s[0, after, :] - xx) + (xy - prior_y(xy, rim(0))) + (xz - prior_z(xz))
+                (s[0, after, :] - xx) + (xy - prior_row(xy, rim(1))) + (xz - prior_z(xz))
             )
             v_out[1, here, :] = v_in[1, here, :] + b * (
-                (xy - s[3, before, :]) + (next_y(yy, rim(2)) - yy) + (yz - prior_z(yz))
+                (xy - s[3, before, :]) + (next_row(yy, rim(0)) - yy) + (yz - prior_z(yz))
             )
             v_out[2, here, :] = v_in[2, here, :] + b * (
-                (xz - s[4, before, :]) + (yz - prior_y(yz, rim(1))) + (next_z(zz) - zz)
+                (xz - s[4, before, :]) + (yz - prior_row(yz, rim(2))) + (next_z(zz) - zz)
             )
             return carry
 
         lax.fori_loop(0, XL, plane, 0)
 
-    loads[0].wait()
-    exchange(v_0, 0, (0, 1), (1, 2), [1], [0, 2])
-    for load in loads[1:4]:
+    for load in loads[:2]:
         load.wait()
-    stress_update(v_0, s_0, 0, s_1, 0)
-    exchange(s_1, 1, (3, 2), (0, 1), [3, 5], [1])
+    moduli[0, pl.ds(YL, ROWS), :] = lame_v[...].astype(F32) * time_step
+    moduli[1, pl.ds(YL, ROWS), :] = shear_v[...].astype(F32) * time_step
+    for load in loads[2:4]:
+        load.wait()
+    for side, rows in enumerate([end_rows, top_rows]):
+        for n in range(3):
+            y_send[side, n] = v_0[n, rows, :]
+        y_send[side, 5] = moduli[1, rows, :]
+    y_send[0, 3] = s_0[3, end_rows, :]
+    y_send[0, 4] = s_0[5, end_rows, :]
+    y_send[1, 3] = s_0[1, top_rows, :]
+    y_send[1, 4] = moduli[0, top_rows, :]
+    pl.semaphore_wait(barrier, GX + GY)
+
+    shears, both, only, one = pl.ds(3, 2), pl.ds(0, 2), pl.ds(0, 1), pl.ds(1, 1)
+    copies = exchange(
+        0,
+        v_0,
+        y_send,
+        y_recv,
+        [
+            (s_0.at[shears, last], s_0.at[shears, below], (next_gx, gy)),
+            (s_0.at[only, first], s_0.at[only, above], (prior_gx, gy)),
+            (moduli.at[one, last], moduli.at[one, below], (next_gx, gy)),
+            (moduli.at[both, first], moduli.at[both, above], (prior_gx, gy)),
+        ],
+    )
+    stress_inside(v_0, s_0, s_1)
+    arrive(0, copies, v_0, y_recv, 6)
+    stress_rims(v_0, s_0, s_1, y_recv, 0)
     loads[4].wait()
-    velocity_update(v_0, s_1, v_1, 1)
-    exchange(v_1, 2, (0, 1), (1, 2), [1], [0, 2])
-    stress_update(v_1, s_1, YL, s_2, 2)
-    exchange(s_2, 3, (3, 2), (0, 1), [3, 5], [1])
-    velocity_update(v_1, s_2, v_2, 3)
+    velocity_update(v_0, s_1, v_1)
+    for side, rows in enumerate([end_rows, top_rows]):
+        for n in range(3):
+            y_send_2[side, n] = v_1[n, rows, :]
+    copies = exchange(1, v_1, y_send_2, y_recv_2, [])
+    stress_inside(v_1, s_1, s_1)
+    arrive(1, copies, v_1, y_recv_2, 3)
+    stress_rims(v_1, s_1, s_1, y_recv_2, 1)
+    velocity_update(v_1, s_1, v_2)
 
     for load in loads[5:8]:
         load.wait()
@@ -569,6 +671,8 @@
     image_p[...] = total_p
     image_s[...] = total_s
 
+    for copy in sent:
+        copy.wait_send()
     for field in range(3):
         wait_gy(field, z_send, gy_send, 0)
         wait_gy(field, z_send_2, gy_send, 1)
@@ -577,26 +681,28 @@
 
 
 def shards(small, large, turns, velocity, stress, lame, shear, buoy, source_p, source_s):
-    any_space = pl.BlockSpec(memory_space=pl.ANY)
+    in_place = pl.BlockSpec(memory_space=pltpu.HBM)
     padded = (XL + 2) * YL
     dma = pltpu.SemaphoreType.DMA
     scratch = [
         *[pltpu.VMEM((3, padded, NZ), F32)] * 3,
-        pltpu.VMEM((6, ROWS, NZ), F32),
         *[pltpu.VMEM((6, padded, NZ), F32)] * 2,
+        pltpu.VMEM((3, XL, NZ), F32),
         *[pltpu.VMEM((ROWS, NZ), BF16)] * 3,
         *[pltpu.VMEM((3, ROWS, NZ), BF16)] * 2,
         pltpu.VMEM(small.shape, BF16),
         pltpu.VMEM(large.shape, BF16),
         pltpu.VMEM(turns.shape, F32),
-        *[pltpu.VMEM((4, 3, XL, NZ), F32)] * 2,
+        pltpu.VMEM((2, padded, NZ), F32),
+        *[pltpu.VMEM((2, 6, XL, NZ), F32)] * 2,
+        *[pltpu.VMEM((2, 3, XL, NZ), F32)] * 2,
+        pltpu.VMEM((2, 2, XL, NZ), F32),
         *[pltpu.VMEM((3, NZ, ROWS), F32)] * 2,
         *[pltpu.VMEM((8 * GX, NZ), F32)] * 4,
         *[pltpu.VMEM((3, NZ, ROWS), F32)] * 2,
         dma((10,)),
-        dma((1,)),
-        dma((4, 4)),
-        dma((4, 4)),
+        dma((2, 10)),
+        dma((2, 10)),
         dma((2, 3)),
         dma((2, 3)),
         dma((2,)),
@@ -606,11 +712,11 @@
     outs = pl.pallas_call(
         kernel,
         out_shape=(out, out),
-        in_specs=[any_space] * 10,
+        in_specs=[in_place] * 10,
         out_specs=(pl.BlockSpec(memory_space=pltpu.VMEM),) * 2,
         scratch_shapes=scratch,
         compiler_params=pltpu.CompilerParams(
-            collective_id=0, has_side_effects=True, vmem_limit_bytes=40 * 2**20
+            collective_id=0, has_side_effects=True, vmem_limit_bytes=60 * 2**20
         ),
     )(
         velocity.reshape(3, ROWS, NZ),

time: 99.6 us -> 79.8 us (0.80)
  the two profiles are of different devices: /device:TPU:1 before, /device:TPU:16 now
where the time goes in v2:
time: 79.8 us; the launch traced here: 79.7 us
  Pallas kernels  75.9 us (95%)
  local copies, waits for them, and re-layouts  3.14 us (4%)
    pallas_call x1, Pallas kernels, shards(): pl.pallas_call(kernel, out_shape=(out, out), in_specs=[in_place] * 10, ou...  75.9 us
    unnamed x2, local copies, waits for them, and re-layouts  3.14 us

profile of v2, /device:TPU:16, one launch (start us, length us, event | category | flops | bytes accessed | tf_op | source)
XLA Modules:
  0.0 79.7 jit_solution(17302275444335524987)
XLA Ops:
  0.6 75.9 %shard_map.113 = (f32[256,128]{1,0:T(8,128)}, f32[256,128]{1,0:T(8,128)}) custom-call(f32[3,256,128]{2,1,0:T(8,128)} %bitcast.10, f32[6,256,128]{2,1,0:T(8,128)} %bitcast.9, bf16[256,128]{1,0:T(8,128)(2,1)} %bitcast.15, bf16[256,128]{1,0:T(8,128)(2,1)} %bitcast.16, bf16[256,128]{1,0:T(8,128)(2,1)} %bitcast.17, bf16[3,256,128]{2,1,0:T(8,128)(2,1)} %bitcast.11, ...), custom_call_target="tpu_custom_call" | custom-call | tf_op jit(solution)/shard_map/pallas_call | solution.py:712
  76.5 1.6 %copy.14 = f32[8,32,128]{2,1,0:T(8,128)} copy(f32[8,32,128]{2,1,0:T(8,128)} %bitcast.14) | data formatting | bytes 262144
  78.1 1.6 %copy.15 = f32[8,32,128]{2,1,0:T(8,128)} copy(f32[8,32,128]{2,1,0:T(8,128)} %bitcast.13) | data formatting | bytes 262144

commit v3 on v2

--- a/solution.py
+++ b/solution.py
@@ -35,15 +35,13 @@
 
 def tables():
     z = np.arange(NZ)
-    per = NZ // 2 // GY
     forward_z = np.zeros((NZ, NZ))
     weighted_z = np.zeros((NZ, NZ))
     back_z = np.zeros((NZ, NZ))
     weighted_back = np.zeros((NZ, NZ))
     norm = 1.0 / (NX * NY * NZ)
     for column in range(NZ // 2):
-        real_row = (column // per) * 2 * per + column % per
-        imag_row = real_row + per
+        real_row, imag_row = column, NZ // 2 + column
         angle = 2 * math.pi * (column * z % NZ) / NZ
         cosine, sine = np.cos(angle), np.sin(angle)
         if column == 0:
@@ -58,14 +56,9 @@
         weighted_back[real_row] = column * back_z[real_row]
         weighted_back[imag_row] = column * back_z[imag_row]
 
-    device_y = np.kron(dft(GY, -1), np.eye(per))
-    arrive = np.zeros((NZ, NZ))
-    for source in range(GY):
-        for part in range(2):
-            for j in range(per):
-                arrive[part * 64 + source * per + j, source * 2 * per + part * per + j] = 1.0
-    left_y = left_form(device_y) @ arrive
-    left_y_back = arrive.T @ left_form(device_y.conj())
+    per = NX // 64
+    left_y = left_form(np.kron(dft(GY, -1), np.eye(per)))
+    left_y_back = left_form(np.kron(dft(GY, 1), np.eye(per)))
     q1 = np.arange(64) // per
     yl = np.arange(ROWS) % YL
     turn_y = np.exp(-2j * math.pi * (np.outer(q1, yl) % NY) / NY)
@@ -171,77 +164,68 @@
     return lax.broadcasted_iota(jnp.int32, (64, 256), axis)
 
 
-def wave_y_rows():
-    return signed(iota(0) // 8 + 8 * (iota(1) % YL), NY)
-
-
-def waves_here(gx, gy):
+def wave_x_of(first, rows):
     lane = iota(1)
-    k2 = lane // 128 + 2 * (lane % 128 // YL)
-    wave_x = signed(iota(0) + 64 * k2, NX)
-    wave_y = signed(gx // 8 + 8 * (lane % YL), NY)
-    wave_z = (gy * 8 + gx % 8).astype(F32)
+    return signed(first + rows + 64 * (lane // 128 + 2 * (lane % 128 // YL)), NX)
+
+
+def waves_here(place, column):
+    wave_x = wave_x_of(place * 8, iota(0) % 8)
+    wave_y = signed(iota(0) // 8 + 8 * (iota(1) % YL), NY)
+    wave_z = column.astype(F32)
     size = wave_x * wave_x + wave_y * wave_y + wave_z * wave_z
-    return wave_x, 1.0 / jnp.maximum(size, 1.0)
-
-
-def x_stage(planes, left, left_back, local, local_back, cosine, sine, wave_x, inverse):
-    stacked = jnp.concatenate(
+    return wave_y, 1.0 / jnp.maximum(size, 1.0)
+
+
+def rows_of(value, n):
+    return value[n * 64 : n * 64 + 64]
+
+
+def x_forward(fields, left, local, cosine, sine):
+    stacked = [
+        jnp.concatenate([planes[h], planes[2 + h]], axis=0) for planes in fields for h in range(2)
+    ]
+    out = matmul(left, jnp.concatenate(stacked, axis=1))
+    even, odd = [], []
+    for n in range(len(fields)):
+        block = out[:, n * 256 : n * 256 + 256]
+        pair = turned(block[:64], block[64:], cosine, sine, False)
+        even.append(jnp.concatenate([lanes(v, 0) + lanes(v, 1) for v in pair], axis=1))
+        odd.append(jnp.concatenate([lanes(v, 0) - lanes(v, 1) for v in pair], axis=1))
+    both = [matmul(jnp.concatenate(v, axis=0), t) for v, t in zip((even, odd), local)]
+    return [
         [
-            jnp.concatenate([planes[2 * f][h], planes[2 * f + 1][h]], axis=0)
-            for f in range(2)
-            for h in range(2)
-        ],
-        axis=1,
-    )
-    out = matmul(left, stacked)
-    fields = []
-    for f in range(2):
-        re, im = out[:64, f * 256 : f * 256 + 256], out[64:, f * 256 : f * 256 + 256]
-        fields.append(turned(re, im, cosine, sine, False))
-    spectra = [[], []]
-    for a in range(2):
-        rows = []
-        for re, im in fields:
-            if a == 0:
-                re, im = lanes(re, 0) + lanes(re, 1), lanes(im, 0) + lanes(im, 1)
-            else:
-                re, im = lanes(re, 0) - lanes(re, 1), lanes(im, 0) - lanes(im, 1)
-            rows.append(jnp.concatenate([re, im], axis=1))
-        got = matmul(jnp.concatenate(rows, axis=0), local[a])
-        wave = lanes(wave_x, a)
-        scale = lanes(inverse, a)
-        phi_re = (wave * got[:64, :128] + got[64:, :128]) * scale
-        phi_im = (wave * got[:64, 128:] + got[64:, 128:]) * scale
-        both = jnp.concatenate(
-            [
-                jnp.concatenate([wave * phi_re, wave * phi_im], axis=1),
-                jnp.concatenate([phi_re, phi_im], axis=1),
-            ],
-            axis=0,
+            jnp.concatenate([lanes(rows_of(v, n), part) for v in both], axis=1)
+            for part in range(2)
+        ]
+        for n in range(len(fields))
+    ]
+
+
+def x_backward(pairs, left, local, cosine, sine):
+    zero, one = [
+        matmul(
+            jnp.concatenate(
+                [jnp.concatenate([lanes(v, a) for v in pair], axis=1) for pair in pairs], axis=0
+            ),
+            local[a],
         )
-        back = matmul(both, local_back[a])
-        for f in range(2):
-            spectra[a].append((back[f * 64 : f * 64 + 64, :128], back[f * 64 : f * 64 + 64, 128:]))
+        for a in range(2)
+    ]
     stacked = []
-    for f in range(2):
-        zero, one = spectra[0][f], spectra[1][f]
+    for n in range(len(pairs)):
         for h in range(2):
-            if h == 0:
-                re, im = zero[0] + one[0], zero[1] + one[1]
-            else:
-                re, im = zero[0] - one[0], zero[1] - one[1]
-            re, im = turned(re, im, lanes(cosine, h), lanes(sine, h), True)
+            even, odd = rows_of(zero, n), rows_of(one, n)
+            both = even + odd if h == 0 else even - odd
+            re, im = turned(
+                lanes(both, 0), lanes(both, 1), lanes(cosine, h), lanes(sine, h), True
+            )
             stacked.append(jnp.concatenate([re, im], axis=0))
-    out = matmul(left_back, jnp.concatenate(stacked, axis=1))
-    result = []
-    for f in range(2):
-        for part in range(2):
-            rows = out[part * 64 : part * 64 + 64]
-            result.append(
-                [rows[:, (2 * f + h) * 128 : (2 * f + h) * 128 + 128] for h in range(2)]
-            )
-    return result
+    out = matmul(left, jnp.concatenate(stacked, axis=1))
+    return [
+        [lanes(rows_of(out, part), 2 * n + h) for part in range(2) for h in range(2)]
+        for n in range(len(pairs))
+    ]
 
 
 def y_back_left(pair, left, cosine, sine):
@@ -258,8 +242,9 @@
     image_p, image_s,
     v_0, v_1, v_2, s_0, s_1, rims, lame_v, shear_v, buoy_v, source_p_v, source_s_v,
     small_v, large_v, turns_v, moduli, y_send, y_recv, y_send_2, y_recv_2, corners,
-    z_send, z_recv, x_send, x_recv, x_send_2, x_recv_2, z_send_2, z_recv_2,
-    load_sem, halo_send, halo_recv, gy_send, gy_recv, gx_send, gx_recv,
+    waves, z_two, z_one, x_recv, x_send, x_recv_2, x_send_2, z_two_back, z_one_back,
+    x_back, x_home, load_sem, halo_send, halo_recv,
+    two_send, one_send, plane_recv, ring_send, ring_recv,
 ):
     gx, gy = lax.axis_index("gx"), lax.axis_index("gy")
 
@@ -268,21 +253,28 @@
     def greet(device):
         pl.semaphore_signal(barrier, inc=1, device_id=device, device_id_type=MESH)
 
-    def greet_x(k, carry):
-        greet((lax.rem(gx + k, GX), gy))
+    core, place = gx % 2, gy // 2 * 2 + gx % 2
+    column = gy % 2 * 32 + gx // 2
+
+    def in_plane(k, its_core):
+        other = (column + k) % 64
+        return other, (other % 32 * 2 + its_core, gy // 2 * 2 + other // 32)
+
+    def in_ring(k):
+        other = (place + k) % 8
+        return other, (gx // 2 * 2 + other % 2, other // 2 * 2 + gy % 2)
+
+    def greet_plane(k, carry):
+        greet(in_plane(k, 0)[1])
+        greet(in_plane(k, 1)[1])
         return carry
 
-    def greet_y(k, carry):
-        greet((gx, lax.rem(gy + k, GY)))
+    def greet_ring(k, carry):
+        greet(in_ring(k)[1])
         return carry
 
     next_gx, prior_gx = lax.rem(gx + 1, GX), lax.rem(gx + GX - 1, GX)
     next_gy, prior_gy = lax.rem(gy + 1, GY), lax.rem(gy + GY - 1, GY)
-    greet((next_gx, prior_gy))
-    greet((prior_gx, next_gy))
-    lax.fori_loop(1, GY, greet_y, 0)
-    lax.fori_loop(1, GX, greet_x, 0)
-
     def interior(ref):
         return ref.at[:, pl.ds(YL, ROWS)]
 
@@ -301,6 +293,12 @@
     loads = [pltpu.make_async_copy(a, b, load_sem.at[n]) for n, (a, b) in enumerate(loads)]
     for load in loads:
         load.start()
+    lax.fori_loop(1, 64, greet_plane, 0)
+    lax.fori_loop(1, 8, greet_ring, 0)
+    greet((gx, next_gy))
+    greet((gx, prior_gy))
+    greet((next_gx, prior_gy))
+    greet((prior_gx, next_gy))
 
     def send(source, target, device, send_sem, recv_sem):
         copy = pltpu.make_async_remote_copy(
@@ -511,6 +509,14 @@
 
         lax.fori_loop(0, XL, plane, 0)
 
+    wave_x = wave_x_of(0, iota(0))
+    waves[0] = jnp.where(core == 0, wave_x, 1.0)
+    waves[1], waves[2] = waves_here(place, column)
+
+    @pl.when(core == 1)
+    def _():
+        x_recv[:, 1] = jnp.zeros((128, 4, 128), F32)
+
     for load in loads[:2]:
         load.wait()
     moduli[0, pl.ds(YL, ROWS), :] = lame_v[...].astype(F32) * time_step
@@ -525,7 +531,7 @@
     y_send[0, 4] = s_0[5, end_rows, :]
     y_send[1, 3] = s_0[1, top_rows, :]
     y_send[1, 4] = moduli[0, top_rows, :]
-    pl.semaphore_wait(barrier, GX + GY)
+    pl.semaphore_wait(barrier, 126 + 7 + 4)
 
     shears, both, only, one = pl.ds(3, 2), pl.ds(0, 2), pl.ds(0, 1), pl.ds(1, 1)
     copies = exchange(
@@ -563,108 +569,174 @@
     def wide(n):
         return large_v[n, 0], large_v[n, 1]
 
-    def all_to_all_gy(field, sent, received, turn):
-        mine = pl.ds(pl.multiple_of(gy * 16, 16), 16)
-
+    turn_y = turns_v[0], turns_v[1]
+    turn_x = turns_v[2], turns_v[3]
+    mine = gy % 2 * 64 + gx
+
+    def landed(ref, sem):
+        pltpu.make_async_copy(ref, ref, sem).wait()
+
+    def planes_of(value):
+        return [lanes(rows_of(value, part), h) for part in range(2) for h in range(2)]
+
+    for n, plane in enumerate(planes_of(z_forward(v_2[1, pl.ds(YL, ROWS), :], narrow(0)))):
+        z_one[:, n, :] = plane
+
+    def send_one(k, carry):
+        other, device = in_plane(k, 1)
+        send(z_one.at[other], x_recv.at[mine, 0], device, one_send.at[0], plane_recv.at[0])
+        return carry
+
+    lax.fori_loop(1, 64, send_one, 0)
+
+    for slot, field in enumerate([0, 2]):
+        value = z_forward(v_2[field, pl.ds(YL, ROWS), :], narrow(slot))
+        for n, plane in enumerate(planes_of(value)):
+            z_two[:, slot, n, :] = plane
+
+    def send_two(k, carry):
+        other, device = in_plane(k, 0)
+        send(z_two.at[other], x_recv.at[mine], device, two_send.at[0], plane_recv.at[0])
+        return carry
+
+    lax.fori_loop(1, 64, send_two, 0)
+
+    @pl.when(core == 0)
+    def _():
+        send_one(0, 0)
+        x_recv[mine] = z_two[column]
+
+    @pl.when(core == 1)
+    def _():
+        send_two(0, 0)
+        x_recv[mine, 0] = z_one[column]
+
+    @pl.when(core == 0)
+    def _():
+        landed(x_recv.at[pl.ds(0, 127)], plane_recv.at[0])
+
+    @pl.when(core == 1)
+    def _():
+        landed(x_recv.at[pl.ds(0, 127), 0], plane_recv.at[0])
+
+    fields = [
+        [x_recv[pl.ds(64 * z, 64), slot, n, :] for n in range(4)]
+        for z in range(2)
+        for slot in range(2)
+    ]
+    pairs = x_forward(fields, narrow(4), [wide(2), wide(3)], *turn_x)
+    alpha = waves[0]
+    for z in range(2):
+        for part in range(2):
+            value = alpha * pairs[2 * z][part] + pairs[2 * z + 1][part]
+            x_send[:, 2 * part + z] = value.reshape(8, 8, 256)
+
+    def ring_exchange(sending, receiving, turn):
         def one(k, carry):
-            to = lax.rem(gy + k, GY)
+            other, device = in_ring(k)
             send(
-                sent.at[field, pl.ds(pl.multiple_of(to * 16, 16), 16)],
-                received.at[field, mine],
-                (gx, to),
-                gy_send.at[turn, field],
-                gy_recv.at[turn, field],
+                sending.at[other],
+                receiving.at[place],
+                device,
+                ring_send.at[turn],
+                ring_recv.at[turn],
             )
             return carry
 
-        lax.fori_loop(1, GY, one, 0)
-        received[field, mine, :] = sent[field, mine, :]
-
-    def wait_gy(field, received, sems, turn):
-        part = received.at[field, pl.ds(0, 16 * (GY - 1))]
-        pltpu.make_async_copy(part, part, sems.at[turn, field]).wait()
-
-    def all_to_all_gx(sent, received, turn):
-        mine = pl.ds(pl.multiple_of(gx * 8, 8), 8)
-
-        def one(k, carry):
-            to = lax.rem(gx + k, GX)
-            send(
-                sent.at[pl.ds(pl.multiple_of(to * 8, 8), 8)],
-                received.at[mine],
-                (to, gy),
-                gx_send.at[turn],
-                gx_recv.at[turn],
-            )
-            return carry
-
-        lax.fori_loop(1, GX, one, 0)
-        received[mine, :] = sent[mine, :]
-
-    def wait_gx(received, sems, turn):
-        part = received.at[pl.ds(0, 8 * (GX - 1))]
-        pltpu.make_async_copy(part, part, sems.at[turn]).wait()
-
-    turn_y = turns_v[0], turns_v[1]
-    turn_x = turns_v[2], turns_v[3]
-
-    for field in range(3):
-        table = narrow(1 if field == 2 else 0)
-        z_send[field] = z_forward(v_2[field, pl.ds(YL, ROWS), :], table)
-        all_to_all_gy(field, z_send, z_recv, 0)
+        lax.fori_loop(1, 8, one, 0)
+        receiving[place] = sending[place]
+        landed(receiving.at[pl.ds(0, 7)], ring_recv.at[turn])
+
+    ring_exchange(x_send, x_recv_2, 0)
 
     pairs = []
-    for field in range(3):
-        wait_gy(field, z_recv, gy_recv, 0)
-        pairs.append(y_forward_left(z_recv[field], narrow(2), *turn_y))
-    pairs = halves_product(pairs, wide(0))
-    wave_y = wave_y_rows()
-    joined = [wave_y * pairs[1][part] + pairs[2][part] for part in range(2)]
-    for p, value in enumerate([pairs[0][0], pairs[0][1]] + joined):
-        for h in range(2):
-            x_send[pl.ds(2 * p + h, 64, stride=8), :] = lanes(value, h)
-    all_to_all_gx(x_send, x_recv, 0)
-
-    wave_x, inverse = waves_here(gx, gy)
-    wait_gx(x_recv, gx_recv, 0)
-    planes = [[x_recv[pl.ds(2 * p + h, 64, stride=8), :] for h in range(2)] for p in range(4)]
-    planes = x_stage(
-        planes,
-        narrow(4),
-        narrow(5),
-        [wide(2), wide(3)],
-        [wide(4), wide(5)],
-        *turn_x,
-        wave_x,
-        inverse,
-    )
-    for p in range(4):
-        for h in range(2):
-            x_send_2[pl.ds(2 * p + h, 64, stride=8), :] = planes[p][h]
-    all_to_all_gx(x_send_2, x_recv_2, 1)
-
-    wait_gx(x_recv_2, gx_recv, 1)
-    planes = [
-        jnp.concatenate([x_recv_2[pl.ds(2 * p + h, 64, stride=8), :] for h in range(2)], axis=1)
-        for p in range(4)
-    ]
-    pairs = [
-        (planes[0], planes[1]),
-        (wave_y * planes[2], wave_y * planes[3]),
-        (planes[2], planes[3]),
-    ]
-    pairs = halves_product(pairs, wide(1))
-    for field in range(3):
-        z_send_2[field] = y_back_left(pairs[field], narrow(3), *turn_y)
-        all_to_all_gy(field, z_send_2, z_recv_2, 1)
+    for its_core in range(2):
+        arrived = [
+            x_recv_2[2 * x + its_core, 2 * part + z]
+            for part in range(2)
+            for x in range(4)
+            for z in range(2)
+        ]
+        pairs.append(y_forward_left(jnp.concatenate(arrived, axis=0), narrow(2), *turn_y))
+    joined, along_y = halves_product(pairs, wide(0))
+    wave_y, inverse = waves[1], waves[2]
+    phi = [(wave_y * along_y[part] + joined[part]) * inverse for part in range(2)]
+    pairs = halves_product([phi, [wave_y * v for v in phi]], wide(1))
+    for its_core in range(2):
+        value = y_back_left(pairs[its_core], narrow(3), *turn_y)
+        for part in range(2):
+            for x in range(4):
+                for z in range(2):
+                    row = part * 64 + (2 * x + z) * 8
+                    x_send_2[2 * x + its_core, 2 * part + z] = value[row : row + 8]
+    ring_exchange(x_send_2, x_back, 1)
+
+    pairs = []
+    for z in range(2):
+        pair = [x_back[:, 2 * part + z].reshape(64, 256) for part in range(2)]
+        pairs += [[alpha * v for v in pair], pair]
+    planes = x_backward(pairs, narrow(5), [wide(4), wide(5)], *turn_x)
+    for z in range(2):
+        for slot in range(2):
+            for n in range(4):
+                x_home[pl.ds(64 * z, 64), slot, n, :] = planes[2 * z + slot][n]
+
+    @pl.when(core == 0)
+    def _():
+        def home(its_core):
+            def one(k, carry):
+                other, device = in_plane(k, its_core)
+                source = x_home.at[other // 32 * 64 + device[0]]
+                send(source, z_two_back.at[column], device, two_send.at[1], plane_recv.at[1])
+                return carry
+
+            return one
+
+        lax.fori_loop(1, 64, home(0), 0)
+        lax.fori_loop(0, 64, home(1), 0)
+        z_two_back[column] = x_home[mine]
+
+    @pl.when(core == 1)
+    def _():
+        def home(its_core):
+            def one(k, carry):
+                other, device = in_plane(k, its_core)
+                source = x_home.at[other // 32 * 64 + device[0], 0]
+                send(source, z_one_back.at[column], device, one_send.at[1], plane_recv.at[2])
+                return carry
+
+            return one
+
+        lax.fori_loop(1, 64, home(1), 0)
+        lax.fori_loop(0, 64, home(0), 0)
+        z_one_back[column] = x_home[mine, 0]
 
     for load in loads[8:]:
         load.wait()
+
+    @pl.when(core == 0)
+    def _():
+        landed(z_two_back.at[pl.ds(0, 63)], plane_recv.at[1])
+        landed(z_one_back, plane_recv.at[2])
+
+    @pl.when(core == 1)
+    def _():
+        landed(z_two_back, plane_recv.at[1])
+        landed(z_one_back.at[pl.ds(0, 63)], plane_recv.at[2])
+
+    def column_rows(planes):
+        halves = [jnp.concatenate(planes[2 * p : 2 * p + 2], axis=1) for p in range(2)]
+        return jnp.concatenate(halves, axis=0)
+
+    gathered = [
+        column_rows([z_two_back[:, 0, n, :] for n in range(4)]),
+        column_rows([z_one_back[:, n, :] for n in range(4)]),
+        column_rows([z_two_back[:, 1, n, :] for n in range(4)]),
+    ]
     total_p = jnp.zeros((ROWS, NZ), F32)
     total_s = jnp.zeros((ROWS, NZ), F32)
     for field in range(3):
-        wait_gy(field, z_recv_2, gy_recv, 1)
-        p_field = z_back(z_recv_2[field], narrow(7 if field == 2 else 6))
+        p_field = z_back(gathered[field], narrow(7 if field == 2 else 6))
         s_field = v_2[field, pl.ds(YL, ROWS), :] - p_field
         total_p += source_p_v[field].astype(F32) * p_field
         total_s += source_s_v[field].astype(F32) * s_field
@@ -673,11 +745,20 @@
 
     for copy in sent:
         copy.wait_send()
-    for field in range(3):
-        wait_gy(field, z_send, gy_send, 0)
-        wait_gy(field, z_send_2, gy_send, 1)
-    wait_gx(x_send, gx_send, 0)
-    wait_gx(x_send_2, gx_send, 1)
+    landed(x_send.at[pl.ds(0, 7)], ring_send.at[0])
+    landed(x_send_2.at[pl.ds(0, 7)], ring_send.at[1])
+
+    @pl.when(core == 0)
+    def _():
+        landed(z_two.at[pl.ds(0, 63)], two_send.at[0])
+        landed(z_one, one_send.at[0])
+        landed(x_home.at[pl.ds(0, 127)], two_send.at[1])
+
+    @pl.when(core == 1)
+    def _():
+        landed(z_two, two_send.at[0])
+        landed(z_one.at[pl.ds(0, 63)], one_send.at[0])
+        landed(x_home.at[pl.ds(0, 127), 0], one_send.at[1])
 
 
 def shards(small, large, turns, velocity, stress, lame, shear, buoy, source_p, source_s):
@@ -697,14 +778,21 @@
         *[pltpu.VMEM((2, 6, XL, NZ), F32)] * 2,
         *[pltpu.VMEM((2, 3, XL, NZ), F32)] * 2,
         pltpu.VMEM((2, 2, XL, NZ), F32),
-        *[pltpu.VMEM((3, NZ, ROWS), F32)] * 2,
-        *[pltpu.VMEM((8 * GX, NZ), F32)] * 4,
-        *[pltpu.VMEM((3, NZ, ROWS), F32)] * 2,
+        pltpu.VMEM((3, 64, 256), F32),
+        pltpu.VMEM((64, 2, 4, 128), F32),
+        pltpu.VMEM((64, 4, 128), F32),
+        pltpu.VMEM((128, 2, 4, 128), F32),
+        *[pltpu.VMEM((8, 4, 8, 256), F32)] * 3,
+        pltpu.VMEM((64, 2, 4, 128), F32),
+        pltpu.VMEM((64, 4, 128), F32),
+        pltpu.VMEM((8, 4, 8, 256), F32),
+        pltpu.VMEM((128, 2, 4, 128), F32),
         dma((10,)),
         dma((2, 10)),
         dma((2, 10)),
-        dma((2, 3)),
-        dma((2, 3)),
+        dma((2,)),
+        dma((2,)),
+        dma((3,)),
         dma((2,)),
         dma((2,)),
     ]

time: 79.8 us -> 78.1 us (0.979)
  the two profiles are of different devices: /device:TPU:16 before, /device:TPU:1 now
where the time goes in v3:
time: 78.1 us; the launch traced here: 78 us
  Pallas kernels  74.2 us (95%)
  local copies, waits for them, and re-layouts  3.14 us (4%)
    pallas_call x1, Pallas kernels, shards(): pl.pallas_call(kernel, out_shape=(out, out), in_specs=[in_place] * 10, ou...  74.2 us
    unnamed x2, local copies, waits for them, and re-layouts  3.14 us

profile of v3, /device:TPU:1, one launch (start us, length us, event | category | flops | bytes accessed | tf_op | source)
XLA Modules:
  0.0 78.0 jit_solution(16024802502289986503)
XLA Ops:
  0.6 74.2 %shard_map.113 = (f32[256,128]{1,0:T(8,128)}, f32[256,128]{1,0:T(8,128)}) custom-call(f32[3,256,128]{2,1,0:T(8,128)} %bitcast.10, f32[6,256,128]{2,1,0:T(8,128)} %bitcast.9, bf16[256,128]{1,0:T(8,128)(2,1)} %bitcast.15, bf16[256,128]{1,0:T(8,128)(2,1)} %bitcast.16, bf16[256,128]{1,0:T(8,128)(2,1)} %bitcast.17, bf16[3,256,128]{2,1,0:T(8,128)(2,1)} %bitcast.11, ...), custom_call_target="tpu_custom_call" | custom-call | tf_op jit(solution)/shard_map/pallas_call | solution.py:800
  74.9 1.6 %copy.14 = f32[8,32,128]{2,1,0:T(8,128)} copy(f32[8,32,128]{2,1,0:T(8,128)} %bitcast.14) | data formatting | bytes 262144
  76.4 1.6 %copy.15 = f32[8,32,128]{2,1,0:T(8,128)} copy(f32[8,32,128]{2,1,0:T(8,128)} %bitcast.13) | data formatting | bytes 262144

commit v4 on v3

--- a/solution.py
+++ b/solution.py
@@ -483,31 +483,56 @@
         old = y_recv[0, 4] if turn == 0 else rims[2]
         rims[2] = old + mu * ((next_z(v_y) - v_y) + (v[2, top_rows, :] - v_z))
 
-    def velocity_update(v_in, s, v_out):
-        def plane(i, carry):
-            here = pl.ds(pl.multiple_of((i + 1) * YL, YL), YL)
-            before = pl.ds(pl.multiple_of(i * YL, YL), YL)
-            after = pl.ds(pl.multiple_of((i + 2) * YL, YL), YL)
-            inner = pl.ds(pl.multiple_of(i * YL, YL), YL)
-
-            def rim(n):
-                return rims[n, pl.ds(i, 1), :]
-
-            b = buoy_v[inner, :].astype(F32) * time_step
-            xx, yy, zz = s[0, here, :], s[1, here, :], s[2, here, :]
-            xy, xz, yz = s[3, here, :], s[4, here, :], s[5, here, :]
-            v_out[0, here, :] = v_in[0, here, :] + b * (
-                (s[0, after, :] - xx) + (xy - prior_row(xy, rim(1))) + (xz - prior_z(xz))
+    def velocity_plane(v_in, s, v_out, i):
+        here = pl.ds(plane_at((i + 1) * YL), YL)
+        before = pl.ds(plane_at(i * YL), YL)
+        after = pl.ds(plane_at((i + 2) * YL), YL)
+        rim_yy, rim_xy, rim_yz = 0.0, 0.0, 0.0
+        if isinstance(i, int):
+            rim_yy, rim_xy, rim_yz = [rims[n, pl.ds(i, 1), :] for n in range(3)]
+        b = moduli[2, here, :]
+        xx, yy, zz = s[0, here, :], s[1, here, :], s[2, here, :]
+        xy, xz, yz = s[3, here, :], s[4, here, :], s[5, here, :]
+        v_out[0, here, :] = v_in[0, here, :] + b * (
+            (s[0, after, :] - xx) + (xy - prior_row(xy, rim_xy)) + (xz - prior_z(xz))
+        )
+        v_out[1, here, :] = v_in[1, here, :] + b * (
+            (xy - s[3, before, :]) + (next_row(yy, rim_yy) - yy) + (yz - prior_z(yz))
+        )
+        v_out[2, here, :] = v_in[2, here, :] + b * (
+            (xz - s[4, before, :]) + (yz - prior_row(yz, rim_yz)) + (next_z(zz) - zz)
+        )
+
+    def velocity_inside(v_in, s, v_out):
+        def middle(i, carry):
+            velocity_plane(v_in, s, v_out, i)
+            return carry
+
+        lax.fori_loop(1, XL - 1, middle, 0)
+
+    def velocity_rims(v_in, s, v_out):
+        velocity_plane(v_in, s, v_out, 0)
+        velocity_plane(v_in, s, v_out, XL - 1)
+        for row in (0, YL - 1):
+            rows = pl.ds(YL + row, XL, stride=YL)
+            beside = pl.ds(YL + row + (1 if row == 0 else -1), XL, stride=YL)
+            over, under = pl.ds(ROWS + YL + row, 1), pl.ds(row, 1)
+            b = moduli[2, rows, :]
+            xx, yy, zz = s[0, rows, :], s[1, rows, :], s[2, rows, :]
+            xy, xz, yz = s[3, rows, :], s[4, rows, :], s[5, rows, :]
+            if row == 0:
+                xy_prior, yz_prior, yy_next = rims[1], rims[2], s[1, beside, :]
+            else:
+                xy_prior, yz_prior, yy_next = s[3, beside, :], s[5, beside, :], rims[0]
+            v_out[0, rows, :] = v_in[0, rows, :] + b * (
+                (next_row(xx, s[0, over, :]) - xx) + (xy - xy_prior) + (xz - prior_z(xz))
             )
-            v_out[1, here, :] = v_in[1, here, :] + b * (
-                (xy - s[3, before, :]) + (next_row(yy, rim(0)) - yy) + (yz - prior_z(yz))
+            v_out[1, rows, :] = v_in[1, rows, :] + b * (
+                (xy - prior_row(xy, s[3, under, :])) + (yy_next - yy) + (yz - prior_z(yz))
             )
-            v_out[2, here, :] = v_in[2, here, :] + b * (
-                (xz - s[4, before, :]) + (yz - prior_row(yz, rim(2))) + (next_z(zz) - zz)
+            v_out[2, rows, :] = v_in[2, rows, :] + b * (
+                (xz - prior_row(xz, s[4, under, :])) + (yz - yz_prior) + (next_z(zz) - zz)
             )
-            return carry
-
-        lax.fori_loop(0, XL, plane, 0)
 
     wave_x = wave_x_of(0, iota(0))
     waves[0] = jnp.where(core == 0, wave_x, 1.0)
@@ -547,18 +572,21 @@
         ],
     )
     stress_inside(v_0, s_0, s_1)
+    loads[4].wait()
+    moduli[2, pl.ds(YL, ROWS), :] = buoy_v[...].astype(F32) * time_step
+    velocity_inside(v_0, s_1, v_1)
     arrive(0, copies, v_0, y_recv, 6)
     stress_rims(v_0, s_0, s_1, y_recv, 0)
-    loads[4].wait()
-    velocity_update(v_0, s_1, v_1)
+    velocity_rims(v_0, s_1, v_1)
     for side, rows in enumerate([end_rows, top_rows]):
         for n in range(3):
             y_send_2[side, n] = v_1[n, rows, :]
     copies = exchange(1, v_1, y_send_2, y_recv_2, [])
     stress_inside(v_1, s_1, s_1)
+    velocity_inside(v_1, s_1, v_2)
     arrive(1, copies, v_1, y_recv_2, 3)
     stress_rims(v_1, s_1, s_1, y_recv_2, 1)
-    velocity_update(v_1, s_1, v_2)
+    velocity_rims(v_1, s_1, v_2)
 
     for load in loads[5:8]:
         load.wait()
@@ -671,72 +699,82 @@
                     x_send_2[2 * x + its_core, 2 * part + z] = value[row : row + 8]
     ring_exchange(x_send_2, x_back, 1)
 
-    pairs = []
+    def home(z, its_core, wide_one):
+        def one(k, carry):
+            chip = (gx // 2 + k) % 32
+            device = (chip * 2 + its_core, gy // 2 * 2 + z)
+            if wide_one:
+                source = x_home.at[z * 64 + device[0]]
+                send(source, z_two_back.at[column], device, two_send.at[1], plane_recv.at[1])
+            else:
+                source = x_home.at[z * 64 + device[0], 0]
+                send(source, z_one_back.at[column], device, one_send.at[1], plane_recv.at[2])
+            return carry
+
+        return one
+
     for z in range(2):
         pair = [x_back[:, 2 * part + z].reshape(64, 256) for part in range(2)]
-        pairs += [[alpha * v for v in pair], pair]
-    planes = x_backward(pairs, narrow(5), [wide(4), wide(5)], *turn_x)
-    for z in range(2):
+        pairs = [[alpha * v for v in pair], pair]
+        planes = x_backward(pairs, narrow(5), [wide(4), wide(5)], *turn_x)
         for slot in range(2):
             for n in range(4):
-                x_home[pl.ds(64 * z, 64), slot, n, :] = planes[2 * z + slot][n]
+                x_home[pl.ds(64 * z, 64), slot, n, :] = planes[slot][n]
+        for its_core in range(2):
+
+            @pl.when(core == its_core)
+            def _():
+                same, other = home(z, its_core, its_core == 0), home(z, 1 - its_core, its_core == 0)
+                lax.fori_loop(1, 32, same, 0)
+                lax.fori_loop(1, 32, other, 0)
+                other(0, 0)
+
+                @pl.when(gy % 2 != z)
+                def _():
+                    same(0, 0)
 
     @pl.when(core == 0)
     def _():
-        def home(its_core):
-            def one(k, carry):
-                other, device = in_plane(k, its_core)
-                source = x_home.at[other // 32 * 64 + device[0]]
-                send(source, z_two_back.at[column], device, two_send.at[1], plane_recv.at[1])
-                return carry
-
-            return one
-
-        lax.fori_loop(1, 64, home(0), 0)
-        lax.fori_loop(0, 64, home(1), 0)
         z_two_back[column] = x_home[mine]
 
     @pl.when(core == 1)
     def _():
-        def home(its_core):
-            def one(k, carry):
-                other, device = in_plane(k, its_core)
-                source = x_home.at[other // 32 * 64 + device[0], 0]
-                send(source, z_one_back.at[column], device, one_send.at[1], plane_recv.at[2])
-                return carry
-
-            return one
-
-        lax.fori_loop(1, 64, home(1), 0)
-        lax.fori_loop(0, 64, home(0), 0)
         z_one_back[column] = x_home[mine, 0]
 
     for load in loads[8:]:
         load.wait()
-
-    @pl.when(core == 0)
-    def _():
-        landed(z_two_back.at[pl.ds(0, 63)], plane_recv.at[1])
-        landed(z_one_back, plane_recv.at[2])
-
-    @pl.when(core == 1)
-    def _():
-        landed(z_two_back, plane_recv.at[1])
-        landed(z_one_back.at[pl.ds(0, 63)], plane_recv.at[2])
 
     def column_rows(planes):
         halves = [jnp.concatenate(planes[2 * p : 2 * p + 2], axis=1) for p in range(2)]
         return jnp.concatenate(halves, axis=0)
 
-    gathered = [
-        column_rows([z_two_back[:, 0, n, :] for n in range(4)]),
-        column_rows([z_one_back[:, n, :] for n in range(4)]),
-        column_rows([z_two_back[:, 1, n, :] for n in range(4)]),
-    ]
     total_p = jnp.zeros((ROWS, NZ), F32)
     total_s = jnp.zeros((ROWS, NZ), F32)
-    for field in range(3):
-        p_field = z_back(gathered[field], narrow(7 if field == 2 else 6))
+    for field in (1, 0, 2):
+        if field == 1:
+
+            @pl.when(core == 0)
+            def _():
+                landed(z_one_back, plane_recv.at[2])
+
+            @pl.when(core == 1)
+            def _():
+                landed(z_one_back.at[pl.ds(0, 63)], plane_recv.at[2])
+
+            planes = [z_one_back[:, n, :] for n in range(4)]
+        else:
+            if field == 0:
+
+                @pl.when(core == 0)
+                def _():
+                    landed(z_two_back.at[pl.ds(0, 63)], plane_recv.at[1])
+
+                @pl.when(core == 1)
+                def _():
+                    landed(z_two_back, plane_recv.at[1])
+
+            planes = [z_two_back[:, field // 2, n, :] for n in range(4)]
+        p_field = z_back(column_rows(planes), narrow(7 if field == 2 else 6))
         s_field = v_2[field, pl.ds(YL, ROWS), :] - p_field
         total_p += source_p_v[field].astype(F32) * p_field
         total_s += source_s_v[field].astype(F32) * s_field
@@ -774,7 +812,7 @@
         pltpu.VMEM(small.shape, BF16),
         pltpu.VMEM(large.shape, BF16),
         pltpu.VMEM(turns.shape, F32),
-        pltpu.VMEM((2, padded, NZ), F32),
+        pltpu.VMEM((3, padded, NZ), F32),
         *[pltpu.VMEM((2, 6, XL, NZ), F32)] * 2,
         *[pltpu.VMEM((2, 3, XL, NZ), F32)] * 2,
         pltpu.VMEM((2, 2, XL, NZ), F32),

time: 78.1 us -> 75.4 us (0.965)
  Pallas kernels: 74.2 us -> 71.4 us
    pallas_call x1, Pallas kernels: 74.2 us -> 71.4 us  [shards(): pl.pallas_call(kernel, out_shape=(out, out), in_specs=[in_place] * 10, ou...]
where the time goes in v4:
time: 75.4 us; the launch traced here: 75.2 us
  Pallas kernels  71.4 us (95%)
  local copies, waits for them, and re-layouts  3.14 us (4%)
    pallas_call x1, Pallas kernels, shards(): pl.pallas_call(kernel, out_shape=(out, out), in_specs=[in_place] * 10, ou...  71.4 us
    unnamed x2, local copies, waits for them, and re-layouts  3.14 us

profile of v4, /device:TPU:1, one launch (start us, length us, event | category | flops | bytes accessed | tf_op | source)
XLA Modules:
  0.0 75.2 jit_solution(18030513154792431309)
XLA Ops:
  0.6 71.4 %shard_map.113 = (f32[256,128]{1,0:T(8,128)}, f32[256,128]{1,0:T(8,128)}) custom-call(f32[3,256,128]{2,1,0:T(8,128)} %bitcast.10, f32[6,256,128]{2,1,0:T(8,128)} %bitcast.9, bf16[256,128]{1,0:T(8,128)(2,1)} %bitcast.15, bf16[256,128]{1,0:T(8,128)(2,1)} %bitcast.16, bf16[256,128]{1,0:T(8,128)(2,1)} %bitcast.17, bf16[3,256,128]{2,1,0:T(8,128)(2,1)} %bitcast.11, ...), custom_call_target="tpu_custom_call" | custom-call | tf_op jit(solution)/shard_map/pallas_call | solution.py:838
  72.1 1.6 %copy.14 = f32[8,32,128]{2,1,0:T(8,128)} copy(f32[8,32,128]{2,1,0:T(8,128)} %bitcast.14) | data formatting | bytes 262144
  73.6 1.6 %copy.15 = f32[8,32,128]{2,1,0:T(8,128)} copy(f32[8,32,128]{2,1,0:T(8,128)} %bitcast.13) | data formatting | bytes 262144

commit v5 on v4

--- a/solution.py
+++ b/solution.py
@@ -127,33 +127,6 @@
     return matmul(table, field, NT)
 
 
-def y_forward_left(arrived, left, cosine, sine):
-    both = matmul(left, arrived)
-    return turned(both[:64], both[64:], cosine, sine, False)
-
-
-def halves_product(pairs, table):
-    stacked = jnp.concatenate(
-        [
-            jnp.concatenate([lanes(re, h), lanes(im, h)], axis=1)
-            for re, im in pairs
-            for h in range(2)
-        ],
-        axis=0,
-    )
-    out = matmul(stacked, table)
-    result = []
-    for n in range(len(pairs)):
-        rows = [out[(2 * n + h) * 64 : (2 * n + h) * 64 + 64] for h in range(2)]
-        result.append(
-            tuple(
-                jnp.concatenate([r[:, part * 128 : part * 128 + 128] for r in rows], axis=1)
-                for part in range(2)
-            )
-        )
-    return result
-
-
 def signed(positions, length):
     half = length // 2
     value = jnp.where(positions < half, positions, positions - length)
@@ -181,7 +154,7 @@
     return value[n * 64 : n * 64 + 64]
 
 
-def x_forward(fields, left, local, cosine, sine):
+def x_forward(fields, left, cosine, sine):
     stacked = [
         jnp.concatenate([planes[h], planes[2 + h]], axis=0) for planes in fields for h in range(2)
     ]
@@ -192,28 +165,13 @@
         pair = turned(block[:64], block[64:], cosine, sine, False)
         even.append(jnp.concatenate([lanes(v, 0) + lanes(v, 1) for v in pair], axis=1))
         odd.append(jnp.concatenate([lanes(v, 0) - lanes(v, 1) for v in pair], axis=1))
-    both = [matmul(jnp.concatenate(v, axis=0), t) for v, t in zip((even, odd), local)]
-    return [
-        [
-            jnp.concatenate([lanes(rows_of(v, n), part) for v in both], axis=1)
-            for part in range(2)
-        ]
-        for n in range(len(fields))
-    ]
-
-
-def x_backward(pairs, left, local, cosine, sine):
-    zero, one = [
-        matmul(
-            jnp.concatenate(
-                [jnp.concatenate([lanes(v, a) for v in pair], axis=1) for pair in pairs], axis=0
-            ),
-            local[a],
-        )
-        for a in range(2)
-    ]
+    return [jnp.concatenate(v, axis=0) for v in (even, odd)]
+
+
+def x_backward(zero, one, left, cosine, sine):
+    count = zero.shape[0] // 64
     stacked = []
-    for n in range(len(pairs)):
+    for n in range(count):
         for h in range(2):
             even, odd = rows_of(zero, n), rows_of(one, n)
             both = even + odd if h == 0 else even - odd
@@ -224,13 +182,8 @@
     out = matmul(left, jnp.concatenate(stacked, axis=1))
     return [
         [lanes(rows_of(out, part), 2 * n + h) for part in range(2) for h in range(2)]
-        for n in range(len(pairs))
+        for n in range(count)
     ]
-
-
-def y_back_left(pair, left, cosine, sine):
-    re, im = turned(pair[0], pair[1], cosine, sine, True)
-    return matmul(left, jnp.concatenate([re, im], axis=0))
 
 
 def z_back(arrived, table):
@@ -652,52 +605,82 @@
         for z in range(2)
         for slot in range(2)
     ]
-    pairs = x_forward(fields, narrow(4), [wide(2), wide(3)], *turn_x)
+    rows = x_forward(fields, narrow(4), *turn_x)
     alpha = waves[0]
-    for z in range(2):
-        for part in range(2):
-            value = alpha * pairs[2 * z][part] + pairs[2 * z + 1][part]
-            x_send[:, 2 * part + z] = value.reshape(8, 8, 256)
-
-    def ring_exchange(sending, receiving, turn):
+
+    def ring_send_half(a, sending, receiving, turn):
         def one(k, carry):
             other, device = in_ring(k)
             send(
-                sending.at[other],
-                receiving.at[place],
+                sending.at[a, other],
+                receiving.at[a, place],
                 device,
-                ring_send.at[turn],
-                ring_recv.at[turn],
+                ring_send.at[turn, a],
+                ring_recv.at[turn, a],
             )
             return carry
 
         lax.fori_loop(1, 8, one, 0)
-        receiving[place] = sending[place]
-        landed(receiving.at[pl.ds(0, 7)], ring_recv.at[turn])
-
-    ring_exchange(x_send, x_recv_2, 0)
-
-    pairs = []
-    for its_core in range(2):
+        receiving[a, place] = sending[a, place]
+
+    def ring_wait_half(a, receiving, turn):
+        landed(receiving.at[a, pl.ds(0, 7)], ring_recv.at[turn, a])
+
+    for a in range(2):
+        got = matmul(rows[a], wide(2 + a))
+        wave = lanes(alpha, a)
+        for z in range(2):
+            pair, other = rows_of(got, 2 * z), rows_of(got, 2 * z + 1)
+            for part in range(2):
+                value = wave * lanes(pair, part) + lanes(other, part)
+                x_send[a, :, 2 * part + z] = value.reshape(8, 8, 128)
+        ring_send_half(a, x_send, x_recv_2, 0)
+
+    cosine, sine = [lanes(v, 0) for v in turn_y]
+    for a in range(2):
+        wave_y, inverse = lanes(waves[1], a), lanes(waves[2], a)
+        ring_wait_half(a, x_recv_2, 0)
         arrived = [
-            x_recv_2[2 * x + its_core, 2 * part + z]
-            for part in range(2)
-            for x in range(4)
-            for z in range(2)
+            jnp.concatenate(
+                [
+                    x_recv_2[a, 2 * x + its_core, 2 * part + z]
+                    for part in range(2)
+                    for x in range(4)
+                    for z in range(2)
+                ],
+                axis=0,
+            )
+            for its_core in range(2)
         ]
-        pairs.append(y_forward_left(jnp.concatenate(arrived, axis=0), narrow(2), *turn_y))
-    joined, along_y = halves_product(pairs, wide(0))
-    wave_y, inverse = waves[1], waves[2]
-    phi = [(wave_y * along_y[part] + joined[part]) * inverse for part in range(2)]
-    pairs = halves_product([phi, [wave_y * v for v in phi]], wide(1))
-    for its_core in range(2):
-        value = y_back_left(pairs[its_core], narrow(3), *turn_y)
-        for part in range(2):
-            for x in range(4):
-                for z in range(2):
-                    row = part * 64 + (2 * x + z) * 8
-                    x_send_2[2 * x + its_core, 2 * part + z] = value[row : row + 8]
-    ring_exchange(x_send_2, x_back, 1)
+        out = matmul(narrow(2), jnp.concatenate(arrived, axis=1))
+        stacked = []
+        for n in range(2):
+            block = lanes(out, n)
+            stacked.append(
+                jnp.concatenate(turned(block[:64], block[64:], cosine, sine, False), axis=1)
+            )
+        got = matmul(jnp.concatenate(stacked, axis=0), wide(0))
+        wave = jnp.concatenate([wave_y, wave_y], axis=1)
+        phi = (wave * rows_of(got, 1) + rows_of(got, 0)) * jnp.concatenate([inverse] * 2, axis=1)
+        got = matmul(jnp.concatenate([phi, wave * phi], axis=0), wide(1))
+        stacked = []
+        for n in range(2):
+            block = rows_of(got, n)
+            stacked.append(
+                jnp.concatenate(
+                    turned(lanes(block, 0), lanes(block, 1), cosine, sine, True), axis=0
+                )
+            )
+        out = matmul(narrow(3), jnp.concatenate(stacked, axis=1))
+        for its_core in range(2):
+            for part in range(2):
+                for x in range(4):
+                    for z in range(2):
+                        row = part * 64 + (2 * x + z) * 8
+                        x_send_2[a, 2 * x + its_core, 2 * part + z] = lanes(
+                            out[row : row + 8], its_core
+                        )
+        ring_send_half(a, x_send_2, x_back, 1)
 
     def home(z, its_core, wide_one):
         def one(k, carry):
@@ -713,10 +696,19 @@
 
         return one
 
+    products = []
+    for a in range(2):
+        ring_wait_half(a, x_back, 1)
+        wave = jnp.concatenate([lanes(alpha, a)] * 2, axis=1)
+        stacked = []
+        for z in range(2):
+            pair = [x_back[a, :, 2 * part + z].reshape(64, 128) for part in range(2)]
+            pair = jnp.concatenate(pair, axis=1)
+            stacked += [wave * pair, pair]
+        products.append(matmul(jnp.concatenate(stacked, axis=0), wide(4 + a)))
     for z in range(2):
-        pair = [x_back[:, 2 * part + z].reshape(64, 256) for part in range(2)]
-        pairs = [[alpha * v for v in pair], pair]
-        planes = x_backward(pairs, narrow(5), [wide(4), wide(5)], *turn_x)
+        zero, one = [v[128 * z : 128 * z + 128] for v in products]
+        planes = x_backward(zero, one, narrow(5), *turn_x)
         for slot in range(2):
             for n in range(4):
                 x_home[pl.ds(64 * z, 64), slot, n, :] = planes[slot][n]
@@ -783,8 +775,9 @@
 
     for copy in sent:
         copy.wait_send()
-    landed(x_send.at[pl.ds(0, 7)], ring_send.at[0])
-    landed(x_send_2.at[pl.ds(0, 7)], ring_send.at[1])
+    for a in range(2):
+        landed(x_send.at[a, pl.ds(0, 7)], ring_send.at[0, a])
+        landed(x_send_2.at[a, pl.ds(0, 7)], ring_send.at[1, a])
 
     @pl.when(core == 0)
     def _():
@@ -820,10 +813,10 @@
         pltpu.VMEM((64, 2, 4, 128), F32),
         pltpu.VMEM((64, 4, 128), F32),
         pltpu.VMEM((128, 2, 4, 128), F32),
-        *[pltpu.VMEM((8, 4, 8, 256), F32)] * 3,
+        *[pltpu.VMEM((2, 8, 4, 8, 128), F32)] * 3,
         pltpu.VMEM((64, 2, 4, 128), F32),
         pltpu.VMEM((64, 4, 128), F32),
-        pltpu.VMEM((8, 4, 8, 256), F32),
+        pltpu.VMEM((2, 8, 4, 8, 128), F32),
         pltpu.VMEM((128, 2, 4, 128), F32),
         dma((10,)),
         dma((2, 10)),
@@ -831,8 +824,8 @@
         dma((2,)),
         dma((2,)),
         dma((3,)),
-        dma((2,)),
-        dma((2,)),
+        dma((2, 2)),
+        dma((2, 2)),
     ]
     out = jax.ShapeDtypeStruct((ROWS, NZ), F32)
     outs = pl.pallas_call(

time: 75.4 us -> 74.5 us (0.988)
  Pallas kernels: 71.4 us -> 70.5 us
    pallas_call x1, Pallas kernels: 71.4 us -> 70.5 us  [shards(): pl.pallas_call(kernel, out_shape=(out, out), in_specs=[in_place] * 10, ou...]
where the time goes in v5:
time: 74.5 us; the launch traced here: 74.3 us
  Pallas kernels  70.5 us (95%)
  local copies, waits for them, and re-layouts  3.14 us (4%)
    pallas_call x1, Pallas kernels, shards(): pl.pallas_call(kernel, out_shape=(out, out), in_specs=[in_place] * 10, ou...  70.5 us
    unnamed x2, local copies, waits for them, and re-layouts  3.14 us

profile of v5, /device:TPU:1, one launch (start us, length us, event | category | flops | bytes accessed | tf_op | source)
XLA Modules:
  0.0 74.3 jit_solution(2432386807635977497)
XLA Ops:
  0.6 70.5 %shard_map.113 = (f32[256,128]{1,0:T(8,128)}, f32[256,128]{1,0:T(8,128)}) custom-call(f32[3,256,128]{2,1,0:T(8,128)} %bitcast.10, f32[6,256,128]{2,1,0:T(8,128)} %bitcast.9, bf16[256,128]{1,0:T(8,128)(2,1)} %bitcast.15, bf16[256,128]{1,0:T(8,128)(2,1)} %bitcast.16, bf16[256,128]{1,0:T(8,128)(2,1)} %bitcast.17, bf16[3,256,128]{2,1,0:T(8,128)(2,1)} %bitcast.11, ...), custom_call_target="tpu_custom_call" | custom-call | tf_op jit(solution)/shard_map/pallas_call | solution.py:831
  71.2 1.6 %copy.14 = f32[8,32,128]{2,1,0:T(8,128)} copy(f32[8,32,128]{2,1,0:T(8,128)} %bitcast.14) | data formatting | bytes 262144
  72.7 1.6 %copy.15 = f32[8,32,128]{2,1,0:T(8,128)} copy(f32[8,32,128]{2,1,0:T(8,128)} %bitcast.13) | data formatting | bytes 262144

commit v6 on v5

--- a/solution.py
+++ b/solution.py
@@ -209,18 +209,27 @@
     core, place = gx % 2, gy // 2 * 2 + gx % 2
     column = gy % 2 * 32 + gx // 2
 
-    def in_plane(k, its_core):
-        other = (column + k) % 64
-        return other, (other % 32 * 2 + its_core, gy // 2 * 2 + other // 32)
+    chip_0, row_0, own = gx // 2, gy // 2 * 2, gy % 2
+
+    def over_plane(act):
+        def far(k, carry):
+            act(1 - own, lax.rem(chip_0 + k, 32))
+            return carry
+
+        def near(k, carry):
+            act(own, lax.rem(chip_0 + k, 32))
+            return carry
+
+        lax.fori_loop(0, 32, far, 0)
+        lax.fori_loop(1, 32, near, 0)
 
     def in_ring(k):
         other = (place + k) % 8
         return other, (gx // 2 * 2 + other % 2, other // 2 * 2 + gy % 2)
 
-    def greet_plane(k, carry):
-        greet(in_plane(k, 0)[1])
-        greet(in_plane(k, 1)[1])
-        return carry
+    def greet_plane(z, chip):
+        greet((chip * 2, row_0 + z))
+        greet((chip * 2 + 1, row_0 + z))
 
     def greet_ring(k, carry):
         greet(in_ring(k)[1])
@@ -246,12 +255,12 @@
     loads = [pltpu.make_async_copy(a, b, load_sem.at[n]) for n, (a, b) in enumerate(loads)]
     for load in loads:
         load.start()
-    lax.fori_loop(1, 64, greet_plane, 0)
-    lax.fori_loop(1, 8, greet_ring, 0)
     greet((gx, next_gy))
     greet((gx, prior_gy))
     greet((next_gx, prior_gy))
     greet((prior_gx, next_gy))
+    over_plane(greet_plane)
+    lax.fori_loop(1, 8, greet_ring, 0)
 
     def send(source, target, device, send_sem, recv_sem):
         copy = pltpu.make_async_remote_copy(
@@ -563,33 +572,33 @@
     for n, plane in enumerate(planes_of(z_forward(v_2[1, pl.ds(YL, ROWS), :], narrow(0)))):
         z_one[:, n, :] = plane
 
-    def send_one(k, carry):
-        other, device = in_plane(k, 1)
-        send(z_one.at[other], x_recv.at[mine, 0], device, one_send.at[0], plane_recv.at[0])
-        return carry
-
-    lax.fori_loop(1, 64, send_one, 0)
+    def send_one(z, chip):
+        device = (chip * 2 + 1, row_0 + z)
+        source = z_one.at[z * 32 + chip]
+        send(source, x_recv.at[mine, 0], device, one_send.at[0], plane_recv.at[0])
+
+    over_plane(send_one)
 
     for slot, field in enumerate([0, 2]):
         value = z_forward(v_2[field, pl.ds(YL, ROWS), :], narrow(slot))
         for n, plane in enumerate(planes_of(value)):
             z_two[:, slot, n, :] = plane
 
-    def send_two(k, carry):
-        other, device = in_plane(k, 0)
-        send(z_two.at[other], x_recv.at[mine], device, two_send.at[0], plane_recv.at[0])
-        return carry
-
-    lax.fori_loop(1, 64, send_two, 0)
+    def send_two(z, chip):
+        device = (chip * 2, row_0 + z)
+        source = z_two.at[z * 32 + chip]
+        send(source, x_recv.at[mine], device, two_send.at[0], plane_recv.at[0])
+
+    over_plane(send_two)
 
     @pl.when(core == 0)
     def _():
-        send_one(0, 0)
+        send_one(own, chip_0)
         x_recv[mine] = z_two[column]
 
     @pl.when(core == 1)
     def _():
-        send_two(0, 0)
+        send_two(own, chip_0)
         x_recv[mine, 0] = z_one[column]
 
     @pl.when(core == 0)
@@ -684,8 +693,8 @@
 
     def home(z, its_core, wide_one):
         def one(k, carry):
-            chip = (gx // 2 + k) % 32
-            device = (chip * 2 + its_core, gy // 2 * 2 + z)
+            chip = lax.rem(chip_0 + k, 32)
+            device = (chip * 2 + its_core, row_0 + z)
             if wide_one:
                 source = x_home.at[z * 64 + device[0]]
                 send(source, z_two_back.at[column], device, two_send.at[1], plane_recv.at[1])

time: 74.5 us -> 74.5 us (level)
  no operation moved by 1% of the time
where the time goes in v6:
time: 74.5 us; the launch traced here: 74.3 us
  Pallas kernels  70.5 us (95%)
  local copies, waits for them, and re-layouts  3.14 us (4%)
    pallas_call x1, Pallas kernels, shards(): pl.pallas_call(kernel, out_shape=(out, out), in_specs=[in_place] * 10, ou...  70.5 us
    unnamed x2, local copies, waits for them, and re-layouts  3.14 us

profile of v6, /device:TPU:1, one launch (start us, length us, event | category | flops | bytes accessed | tf_op | source)
XLA Modules:
  0.0 74.3 jit_solution(14028632237394382658)
XLA Ops:
  0.6 70.5 %shard_map.113 = (f32[256,128]{1,0:T(8,128)}, f32[256,128]{1,0:T(8,128)}) custom-call(f32[3,256,128]{2,1,0:T(8,128)} %bitcast.10, f32[6,256,128]{2,1,0:T(8,128)} %bitcast.9, bf16[256,128]{1,0:T(8,128)(2,1)} %bitcast.15, bf16[256,128]{1,0:T(8,128)(2,1)} %bitcast.16, bf16[256,128]{1,0:T(8,128)(2,1)} %bitcast.17, bf16[3,256,128]{2,1,0:T(8,128)(2,1)} %bitcast.11, ...), custom_call_target="tpu_custom_call" | custom-call | tf_op jit(solution)/shard_map/pallas_call | solution.py:840
  71.2 1.6 %copy.14 = f32[8,32,128]{2,1,0:T(8,128)} copy(f32[8,32,128]{2,1,0:T(8,128)} %bitcast.14) | data formatting | bytes 262144
  72.8 1.6 %copy.15 = f32[8,32,128]{2,1,0:T(8,128)} copy(f32[8,32,128]{2,1,0:T(8,128)} %bitcast.13) | data formatting | bytes 262144
